TPU v7x, 128 devices: a whole 4x4x4 slice. The times are simulated.
128 devices in a mesh: grp: 4 (over y), seq: 32 (over x, z, core).
Axes of the slice: x: 4, y: 4, z: 4, core: 2. Of those that a mesh axis runs over, the one named last changes fastest.
Arguments:
- points: bfloat16 [65536, 512], P(('grp', 'seq')), may hold values from -6 to 6
- pattern_first: int32 [1024, 3], P(('grp', 'seq')), may hold values from 0 to 255, as said below
- pattern_second: int32 [1024, 3], P(('grp', 'seq')), may hold values from 0 to 7
- destination: int32 [65536], P(('grp', 'seq')), may hold values from 0 to 65535, as said below
- norm_gains: float32 [4, 512], replicated, may hold values from 0.1 to 1.9
- w_qkv: bfloat16 [2, 512, 1536], replicated
- w_proj: bfloat16 [2, 512, 512], replicated, may hold values from -0.25 to 0.25
- w_up: bfloat16 [2, 512, 2048], replicated, may hold values from -0.25 to 0.25
- w_down: bfloat16 [2, 2048, 512], replicated, may hold values from -0.125 to 0.125
- w_head: bfloat16 [3, 512], replicated, may hold values from -0.25 to 0.25
Outputs:
- features: bfloat16 [65536, 512], P(('grp', 'seq'))
- normals: float32 [3, 65536], P(None, ('grp', 'seq'))
Inputs may be any that keep to these rules, and one draw needn't show every extreme that they name: `pattern_first`: the 24 entries of the patches of one device name at most 2 patches (repeats counted) lying on any one device of the group, and exactly 2 on some device. `destination`: a permutation of the positions; the 512 points of one device place at most 8 points in any one block of 512 consecutive positions of the second order, and exactly 8 in some block for every device.
All inputs are finite; a program needn't handle non-finite values.
Results may differ from a plain program's by a relative error of at most 0.024.
Values may be sent and summed in bfloat16 or wider, within the bound.
A program may use at most 128 MiB of HBM per device.

v0:
```python
import jax
import jax.numpy as jnp
from jax import lax
from jax.sharding import PartitionSpec as P

HEADS = 8
PATCH = 64


def layer_norm(rows, gains):
    values = rows.astype(jnp.float32)
    average = jnp.mean(values, axis=-1, keepdims=True)
    spread = jnp.mean((values - average) ** 2, axis=-1, keepdims=True)
    return ((values - average) * lax.rsqrt(spread + 1e-05) * gains).astype(jnp.bfloat16)


def attend(queries, key_rows, value_rows):
    count = key_rows.shape[0]
    channels = queries.shape[1]
    head_dim = channels // HEADS
    qh = queries.reshape(count, PATCH, HEADS, head_dim)
    kh = key_rows.reshape(count, -1, HEADS, head_dim)
    vh = value_rows.reshape(count, -1, HEADS, head_dim)
    scores = jnp.einsum(
        "nqhd,nkhd->nhqk", qh, kh, preferred_element_type=jnp.float32
    ) * head_dim ** (-0.5)
    probs = jax.nn.softmax(scores, axis=-1).astype(jnp.bfloat16)
    mixed = jnp.einsum("nhqk,nkhd->nqhd", probs, vh, preferred_element_type=jnp.float32)
    return mixed.reshape(count * PATCH, channels).astype(jnp.bfloat16)


def finish(rows, attended, section, norm_gains, w_proj, w_up, w_down):
    first = (
        rows.astype(jnp.float32)
        + jnp.dot(attended, w_proj[section], preferred_element_type=jnp.float32)
    ).astype(jnp.bfloat16)
    hidden = layer_norm(first, norm_gains[2 * section + 1])
    upper = jnp.dot(hidden, w_up[section], preferred_element_type=jnp.float32)
    act = jax.nn.gelu(upper, approximate=False).astype(jnp.bfloat16)
    return (
        first.astype(jnp.float32)
        + jnp.dot(act, w_down[section], preferred_element_type=jnp.float32)
    ).astype(jnp.bfloat16)


def shards(
    points,
    pattern_first,
    pattern_second,
    destination,
    norm_gains,
    w_qkv,
    w_proj,
    w_up,
    w_down,
    w_head,
):
    rows_here, channels = points.shape
    patches = rows_here // PATCH
    normed = layer_norm(points, norm_gains[0])
    proj = jnp.dot(normed, w_qkv[0], preferred_element_type=jnp.float32)
    queries = proj[:, :channels].astype(jnp.bfloat16)
    key_flat = proj[:, channels : 2 * channels].astype(jnp.bfloat16)
    value_flat = proj[:, 2 * channels :].astype(jnp.bfloat16)
    key_own = key_flat.reshape(patches, PATCH, channels)
    value_own = value_flat.reshape(patches, PATCH, channels)
    key_group, value_group = (
        lax.all_gather(key_flat, "seq", axis=0, tiled=True),
        lax.all_gather(value_flat, "seq", axis=0, tiled=True),
    )
    key_chosen = key_group.reshape(-1, PATCH, channels)[pattern_first]
    value_chosen = value_group.reshape(-1, PATCH, channels)[pattern_first]
    key_rows = jnp.concatenate([key_own[:, None], key_chosen], axis=1).reshape(
        patches, -1, channels
    )
    value_rows = jnp.concatenate([value_own[:, None], value_chosen], axis=1).reshape(
        patches, -1, channels
    )
    first = finish(
        points, attend(queries, key_rows, value_rows), 0, norm_gains, w_proj, w_up, w_down
    )
    group_count = lax.axis_size("grp")
    shard_count = lax.axis_size("seq")
    devices = group_count * shard_count
    capacity = 2 * rows_here // devices
    slot_total = devices * capacity
    target = destination // rows_here
    place_at = destination % rows_here
    onehot_dev = (target[:, None] == jnp.arange(devices, dtype=jnp.int32)[None, :]).astype(
        jnp.int32
    )
    earlier = jnp.cumsum(onehot_dev, axis=0) - onehot_dev
    send_rank = jnp.sum(earlier * onehot_dev, axis=1)
    slot_index = target * capacity + send_rank
    row_ids = jnp.arange(rows_here, dtype=jnp.int32)
    slot_ids = jnp.arange(slot_total, dtype=jnp.int32)
    match_send = (slot_index[None, :] == slot_ids[:, None]).astype(jnp.int32)
    filled = jnp.sum(match_send, axis=1)
    source_row = jnp.sum(match_send * row_ids[None, :], axis=1)
    outgoing = first[source_row].reshape(devices, capacity, channels)
    out_places = jnp.where(filled > 0, place_at[source_row], -1).reshape(devices, capacity)
    incoming, in_places = (
        lax.all_to_all(outgoing, ("grp", "seq"), split_axis=0, concat_axis=0, tiled=True),
        lax.all_to_all(out_places, ("grp", "seq"), split_axis=0, concat_axis=0, tiled=True),
    )
    incoming = incoming.reshape(-1, channels)
    in_places = in_places.reshape(-1)
    match_recv = (in_places[None, :] == row_ids[:, None]).astype(jnp.int32)
    pick_slot = jnp.sum(match_recv * slot_ids[None, :], axis=1)
    second = incoming[pick_slot]
    normed_two = layer_norm(second, norm_gains[2])
    proj_two = jnp.dot(normed_two, w_qkv[1], preferred_element_type=jnp.float32)
    queries_two = proj_two[:, :channels].astype(jnp.bfloat16)
    key_two = (
        proj_two[:, channels : 2 * channels].astype(jnp.bfloat16).reshape(patches, PATCH, channels)
    )
    value_two = proj_two[:, 2 * channels :].astype(jnp.bfloat16).reshape(patches, PATCH, channels)
    key_rows_two = jnp.concatenate([key_two[:, None], key_two[pattern_second]], axis=1).reshape(
        patches, -1, channels
    )
    value_rows_two = jnp.concatenate(
        [value_two[:, None], value_two[pattern_second]], axis=1
    ).reshape(patches, -1, channels)
    features = finish(
        second,
        attend(queries_two, key_rows_two, value_rows_two),
        1,
        norm_gains,
        w_proj,
        w_up,
        w_down,
    )
    normals = lax.dot_general(
        w_head, features, (((1,), (1,)), ((), ())), preferred_element_type=jnp.float32
    )
    return (features, normals)


def solution(mesh):
    placed = (
        P(("grp", "seq"), None),
        P(("grp", "seq"), None),
        P(("grp", "seq"), None),
        P(("grp", "seq")),
        P(),
        P(),
        P(),
        P(),
        P(),
        P(),
    )
    return jax.shard_map(
        shards,
        mesh=mesh,
        in_specs=placed,
        out_specs=(P(("grp", "seq"), None), P(None, ("grp", "seq"))),
        check_vma=False,
    )
```

profile of v0, /device:TPU:1, one launch (start us, length us, event | category | flops | bytes accessed | tf_op | source)
XLA Modules:
  0.0 318.5 jit_solution(11026403037342974217)
XLA Ops:
  7.2 0.9 fusion.240
  8.1 1.3 copy.75
  9.7 2.5 convolution_convert_fusion.1
  12.2 1.1 fusion.239
  13.3 0.7 all-gather.5.cloned.1.call-update
  14.7 0.6 convert_reduce_fusion
  15.4 6.9 %gather_fusion.3 = s32[1024]{0:T(1024)S(1)} fusion(s32[512]{0:T(512)S(1)} %get-tuple-element.22, s32[1024]{0:T(1024)S(1)} %broadcast_clamp_fusion), kind=kCustom, calls=%fused_computation.3 | custom fusion | bytes 12288 | tf_op jit(solution)/shard_map/gather | solution.py:101
  22.3 0.7 select_n.61
  23.0 11.8 %all-to-all-start.1 = ((s32[128,1,8]{2,1,0:T(1,128)}), s32[128,1,8]{2,1,0:T(1,128)S(1)}, u32[]{:S(2)}, u32[]{:S(2)}) async-start(s32[128,1,8]{2,1,0:T(1,128)} %bitcast.23), calls=%async_computation.1 | async-start | bytes 131072 | tf_op jit(solution)/shard_map/all_to_all | solution.py:104
  35.0 1.5 reshape.159
  36.5 53.8 %all-gather.3.cloned.1.call-done = bf16[16384,512]{1,0:T(8,128)(2,1)} async-done(((bf16[512,512]{1,0:T(8,128)(2,1)}), bf16[16384,512]{1,0:T(8,128)(2,1)}) %all-gather.3.cloned.1.call-update) | async-done | bytes 16777232 | tf_op jit(solution)/shard_map/all_gather | solution.py:69
  90.3 7.6 %gather_fusion = bf16[24,64,512]{2,1,0:T(8,128)(2,1)} fusion(bf16[256,64,512]{2,1,0:T(8,128)(2,1)} %bitcast.132, s32[1024]{0:T(1024)S(1)} %pad_clamp_fusion.2), kind=kCustom, calls=%fused_computation | custom fusion | bytes 3145824 | tf_op jit(solution)/shard_map/gather | solution.py:72
  98.0 66.7 %all-gather.5.cloned.1.call-done = bf16[16384,512]{1,0:T(8,128)(2,1)} async-done(((bf16[512,512]{1,0:T(8,128)(2,1)}), bf16[16384,512]{1,0:T(8,128)(2,1)}) %all-gather.5.cloned.1.call-update) | async-done | bytes 16777232 | tf_op jit(solution)/shard_map/all_gather | solution.py:68
  164.6 7.6 %gather_fusion.1 = bf16[24,64,512]{2,1,0:T(8,128)(2,1)} fusion(bf16[256,64,512]{2,1,0:T(8,128)(2,1)} %bitcast.133, s32[1024]{0:T(1024)S(1)} %pad_clamp_fusion.2), kind=kCustom, calls=%fused_computation.1 | custom fusion | bytes 3145824 | tf_op jit(solution)/shard_map/gather | solution.py:71
  172.3 1.6 pad_maximum_fusion.1
  173.9 3.7 %reshape_reshape.13 = bf16[8,256,8,64]{3,2,1,0:T(8,128)(2,1)} reshape(bf16[8,4,64,512]{3,2,1,0:T(8,128)(2,1)S(1)} %pad_maximum_fusion.1) | data formatting | bytes 4194304 | tf_op jit(solution)/shard_map/reshape;reshape | solution.py:22
  177.5 4.1 %fusion.14 = f32[8,8,64,256]{3,2,1,0:T(8,128)S(1)} fusion(bf16[8,256,8,64]{3,2,1,0:T(8,128)(2,1)} %reshape_reshape.13, bf16[8,64,8,64]{3,2,1,0:T(8,128)(2,1)} %reshape.159), kind=kOutput, calls=%fused_computation.23 | convolution fusion | flops 134217728 | bytes 6815744 | tf_op jit(solution)/shard_map/nqhd,nkhd->nhqk/dot_general | solution.py:24
  181.6 1.4 fusion.241
  183.0 0.7 copy-done.6
  184.8 3.6 %reshape_reshape.12 = bf16[8,256,8,64]{3,2,1,0:T(8,128)(2,1)} reshape(bf16[8,4,64,512]{3,2,1,0:T(8,128)(2,1)S(1)} %pad_maximum_fusion) | data formatting | bytes 4194304 | tf_op jit(solution)/shard_map/reshape;reshape | solution.py:23
  188.5 13.3 %fusion.75 = bf16[8,64,8,64]{1,3,2,0:T(8,128)(2,1)S(1)} fusion(f32[8,8,64]{2,1,0:T(8,128)S(1)} %fusion.241, bf16[8,256,8,64]{3,2,1,0:T(8,128)(2,1)} %reshape_reshape.12, f32[8,8,64,256]{3,2,1,0:T(8,128)} %copy-done.6), kind=kOutput, calls=%fused_computation.109 | convolution fusion | flops 139727104 | bytes 6832128 | tf_op jit(solution)/shard_map/nhqk,nkhd->nqhd/dot_general | solution.py:28
  201.8 1.0 copy.82
  202.7 0.6 convert_element_type.92
  203.4 1.5 convert_reduce_fusion.3
  205.1 13.9 %fusion.92 = bf16[512,512]{0,1:T(8,128)(2,1)S(1)} fusion(bf16[2,2048,512]{2,1,0:T(8,128)(2,1)} %param.18, bf16[2,512,2048]{2,1,0:T(8,128)(2,1)} %param.17, bf16[512,512]{0,1:T(8,128)(2,1)S(1)} %get-tuple-element.25, f32[512]{0:T(512)S(1)} %bitcast.142, f32[512]{0:T(512)S(1)} %add_rsqrt_fusion.2, f32[512]{0:T(512)S(1)} %broadcast_multiply_fusion.2), kind=kOutput, calls=%fused_computation.112 | convolution fusion | flops 2217738240 | bytes 5773312 | tf_op jit(solution)/shard_map/dot_general | solution.py:42
  219.2 5.1 %gather_fusion.2 = bf16[1024,512]{1,0:T(8,128)(2,1)} fusion(bf16[512,512]{1,0:T(8,128)(2,1)S(1)} %copy.86, s32[1024]{0:T(1024)S(1)} %broadcast_clamp_fusion), kind=kCustom, calls=%fused_computation.2 | custom fusion | bytes 2101248 | tf_op jit(solution)/shard_map/gather | solution.py:100
  224.3 7.3 %all-to-all-start = ((bf16[128,8,512]{2,1,0:T(8,128)(2,1)}), bf16[128,8,512]{2,1,0:T(8,128)(2,1)S(1)}, u32[]{:S(2)}, u32[]{:S(2)}) async-start(bf16[128,8,512]{2,1,0:T(8,128)(2,1)} %bitcast.21), calls=%async_computation | async-start | bytes 2097152 | tf_op jit(solution)/shard_map/all_to_all | solution.py:103
  232.3 0.8 reduce.3
  233.5 17.2 %all-to-all-done = bf16[128,8,512]{2,1,0:T(8,128)(2,1)S(1)} async-done(((bf16[128,8,512]{2,1,0:T(8,128)(2,1)}), bf16[128,8,512]{2,1,0:T(8,128)(2,1)S(1)}, u32[]{:S(2)}, u32[]{:S(2)}) %all-to-all-start) | async-done | bytes 1048608 | tf_op jit(solution)/shard_map/all_to_all | solution.py:103
  250.7 2.0 gather_fusion.4
  253.7 2.5 convolution_convert_fusion
  256.4 1.6 reshape.165
  258.0 1.9 gather_fusion.6
  259.9 1.9 gather_fusion.5
  261.7 1.6 pad_maximum_fusion.2
  263.3 3.7 %reshape_reshape.14 = bf16[8,256,8,64]{3,2,1,0:T(8,128)(2,1)} reshape(bf16[8,4,64,512]{3,2,1,0:T(8,128)(2,1)S(1)} %pad_maximum_fusion.2) | data formatting | bytes 4194304 | tf_op jit(solution)/shard_map/reshape;reshape | solution.py:23
  267.0 1.6 pad_maximum_fusion.3
  268.5 3.6 %reshape_reshape.15 = bf16[8,256,8,64]{3,2,1,0:T(8,128)(2,1)} reshape(bf16[8,4,64,512]{3,2,1,0:T(8,128)(2,1)S(1)} %pad_maximum_fusion.3) | data formatting | bytes 4194304 | tf_op jit(solution)/shard_map/reshape;reshape | solution.py:22
  272.2 4.1 %fusion.10 = f32[8,8,64,256]{3,2,1,0:T(8,128)S(1)} fusion(bf16[8,256,8,64]{3,2,1,0:T(8,128)(2,1)} %reshape_reshape.15, bf16[8,64,8,64]{3,2,1,0:T(8,128)(2,1)} %reshape.165), kind=kOutput, calls=%fused_computation.19 | convolution fusion | flops 134217728 | bytes 6815744 | tf_op jit(solution)/shard_map/nqhd,nkhd->nhqk/dot_general | solution.py:24
  276.3 2.0 copy-done.7
  278.2 1.4 fusion.242
  279.6 13.4 %fusion.72 = bf16[8,64,8,64]{1,3,2,0:T(8,128)(2,1)S(1)} fusion(f32[8,8,64]{2,1,0:T(8,128)S(1)} %fusion.242, bf16[8,256,8,64]{3,2,1,0:T(8,128)(2,1)} %reshape_reshape.14, f32[8,8,64,256]{3,2,1,0:T(8,128)} %copy-done.7), kind=kOutput, calls=%fused_computation.108 | convolution fusion | flops 139727104 | bytes 6832128 | tf_op jit(solution)/shard_map/nhqk,nkhd->nqhd/dot_general | solution.py:28
  293.0 0.9 copy.95
  293.9 0.6 convert_element_type.106
  294.6 1.5 convert_reduce_fusion.1
  296.3 13.4 %fusion.99 = bf16[512,512]{0,1:T(8,128)(2,1)S(1)} fusion(bf16[2,2048,512]{2,1,0:T(8,128)(2,1)} %param.18, bf16[2,512,2048]{2,1,0:T(8,128)(2,1)} %param.17, bf16[512,512]{0,1:T(8,128)(2,1)S(1)} %get-tuple-element.27, f32[512]{0:T(512)S(1)} %bitcast.140, f32[512]{0:T(512)S(1)} %add_rsqrt_fusion, f32[512]{0:T(512)S(1)} %broadcast_multiply_fusion), kind=kOutput, calls=%fused_computation.113 | convolution fusion | flops 2217738240 | bytes 5773312 | tf_op jit(solution)/shard_map/dot_general | solution.py:42
  309.7 1.0 copy.97
  310.7 0.8 convolution_bitcast_fusion
  (69 shorter events, 5.2 us)
Async XLA Ops:
  7.2 303.5 %copy-start = (bf16[3,512]{1,0:T(4,128)(2,1)S(1)}, bf16[3,512]{1,0:T(4,128)(2,1)}, u32[]{:S(2)}) copy-start(bf16[3,512]{1,0:T(4,128)(2,1)} %param.19) | copy-start | bytes 9220
  7.2 83.2 %all-gather.3.cloned.1.call-start = ((), (), s32[]{:S(2)}) async-start(), calls=%async_computation.2 | async-start | bytes 17301504 | tf_op jit(solution)/shard_map/all_gather | solution.py:69
  9.7 4.4 %copy-start.8 = (s32[512]{0:T(512)S(1)}, s32[512]{0:T(512)}, u32[]{:S(2)}) copy-start(s32[512]{0:T(512)} %param.13) | copy-start | bytes 6148
  13.3 21.5 %copy-start.9 = (s32[8,3]{0,1:T(4,128)S(1)}, s32[8,3]{0,1:T(4,128)}, u32[]{:S(2)}) copy-start(s32[8,3]{0,1:T(4,128)} %param.11) | copy-start | bytes 292
  13.3 151.4 %all-gather.5.cloned.1.call-start = ((), (), s32[]{:S(2)}) async-start(), calls=%async_computation.3 | async-start | bytes 17301504 | tf_op jit(solution)/shard_map/all_gather | solution.py:68
  22.3 150.0 %copy-start.5 = (bf16[512,512]{1,0:T(8,128)(2,1)S(1)}, bf16[512,512]{1,0:T(8,128)(2,1)}, u32[]{:S(2)}) copy-start(bf16[512,512]{1,0:T(8,128)(2,1)} %get-tuple-element.16) | copy-start | bytes 1572868
  23.0 201.3 %all-to-all-start.1 = ((s32[128,1,8]{2,1,0:T(1,128)}), s32[128,1,8]{2,1,0:T(1,128)S(1)}, u32[]{:S(2)}, u32[]{:S(2)}) async-start(s32[128,1,8]{2,1,0:T(1,128)} %bitcast.23), calls=%async_computation.1 | async-start | bytes 131072 | tf_op jit(solution)/shard_map/all_to_all | solution.py:104
  181.6 2.1 copy-start.6
  181.6 2.6 copy-start.1
  181.6 3.0 copy-start.4
  219.2 12.4 %copy-start.10 = (s32[8,3]{0,1:T(4,128)S(1)}, s32[8,3]{0,1:T(4,128)}, u32[]{:S(2)}) copy-start(s32[8,3]{0,1:T(4,128)} %param.12) | copy-start | bytes 292
  224.3 26.4 %all-to-all-start = ((bf16[128,8,512]{2,1,0:T(8,128)(2,1)}), bf16[128,8,512]{2,1,0:T(8,128)(2,1)S(1)}, u32[]{:S(2)}, u32[]{:S(2)}) async-start(bf16[128,8,512]{2,1,0:T(8,128)(2,1)} %bitcast.21), calls=%async_computation | async-start | bytes 2097152 | tf_op jit(solution)/shard_map/all_to_all | solution.py:103
  252.9 0.8 copy-start.2
  276.3 2.0 copy-start.7
  279.6 14.9 %copy-start.3 = (bf16[512,512]{0,1:T(8,128)(2,1)S(1)}, bf16[512,512]{0,1:T(8,128)(2,1)}, u32[]{:S(2)}) copy-start(bf16[512,512]{0,1:T(8,128)(2,1)} %copy-done.2) | copy-start | bytes 1572868
Sparse Core Ops, SparseCore 0:
  13.4 76.8 all-gather.2
  92.6 71.9 all-gather.4
where the time goes:
time: 323 us; the launch traced here: 319 us
  waiting for transfers between devices  138 us (43%)
  matrix products  71 us (22%)
  local copies, waits for them, and re-layouts  64.3 us (20%)
  starting transfers between devices  19.1 us (6%)
  between operations  14.6 us (5%)
  other arithmetic  11 us (3%)
    all_gather x1, waiting for transfers between devices, shards(): lax.all_gather(key_flat, 'seq', axis=0, tiled=True)  66.7 us
    all_gather x1, waiting for transfers between devices, shards(): lax.all_gather(value_flat, 'seq', axis=0, tiled=True)  53.8 us
    dot_general x2, matrix products, finish(): jnp.dot(act, w_down[section], preferred_element_type=jnp.float32)  27.3 us
    dot_general x2, matrix products, attend(): jnp.einsum('nhqk,nkhd->nqhd', probs, vh, preferred_element_type=jnp.float32)  26.7 us
    all_to_all x1, waiting for transfers between devices, shards(): lax.all_to_all(outgoing, ('grp', 'seq'), split_axis=0, concat_axis=0, til...  17.2 us
    all_to_all x1, starting transfers between devices, shards(): lax.all_to_all(out_places, ('grp', 'seq'), split_axis=0, concat_axis=0, t...  11.8 us
    dot_general x2, matrix products, attend(): jnp.einsum('nqhd,nkhd->nhqk', qh, kh, preferred_element_type=jnp.float32)  8.16 us
    gather x1, local copies, waits for them, and re-layouts, shards(): key_chosen = key_group.reshape(-1, PATCH, channels)[pattern_first]  7.62 us
  transfers between devices with their start and end apart: 4, of which 3 were waited for; matrix products, arithmetic and copies ran while one was open for 24% of the time, Pallas kernels for 0%

commit v1 on v0

v1 whole, which is shorter than its diff:
```python
import functools

import jax
import jax.numpy as jnp
from jax import lax
from jax.experimental import pallas as pl
from jax.experimental.pallas import tpu as pltpu
from jax.sharding import PartitionSpec as P

HEADS = 8
PATCH = 64
SLOTS = 8
GROUP_HEADS = 4
BF16 = jnp.bfloat16
F32 = jnp.float32


def norm(rows, gains):
    values = rows.astype(F32)
    centered = values - jnp.mean(values, axis=-1, keepdims=True)
    spread = jnp.mean(centered * centered, axis=-1, keepdims=True)
    return (centered * lax.rsqrt(spread + 1e-05) * gains).astype(BF16)


def mm(a, b):
    return jnp.dot(a, b, preferred_element_type=F32)


def attend_patch(queries, keys, values):
    width = GROUP_HEADS * PATCH
    lane = lax.broadcasted_iota(jnp.int32, (PATCH, width), 1) // PATCH
    mixed = []
    for part in range(HEADS // GROUP_HEADS):
        cols = slice(part * width, (part + 1) * width)
        q = queries[:, cols]
        spread = jnp.concatenate(
            [jnp.where(lane == head, q, jnp.zeros_like(q)) for head in range(GROUP_HEADS)], axis=0
        )
        scores = lax.dot_general(
            spread, keys[:, cols], (((1,), (1,)), ((), ())), preferred_element_type=F32
        )
        top = jnp.max(scores, axis=-1, keepdims=True)
        weights = jnp.exp((scores - top) * PATCH ** (-0.5))
        total = jnp.sum(weights, axis=-1, keepdims=True)
        out = mm(weights.astype(BF16), values[:, cols]) * (1.0 / total)
        acc = jnp.where(lane == 0, out[:PATCH], 0.0)
        for head in range(1, GROUP_HEADS):
            acc = acc + jnp.where(lane == head, out[head * PATCH : (head + 1) * PATCH], 0.0)
        mixed.append(acc)
    return jnp.concatenate(mixed, axis=1).astype(BF16)


def finish(rows, att_ref, gains, wp_ref, wu_ref, wd_ref, acc_ref, waits):
    waits[0]()
    first = (rows.astype(F32) + mm(att_ref[...], wp_ref[...])).astype(BF16)
    hidden = norm(first, gains)
    acc_ref[...] = first.astype(F32)
    waits[1]()
    waits[2]()
    ff = wu_ref.shape[1]
    step = 512
    for at in range(0, ff, step):
        upper = mm(hidden, wu_ref[:, at : at + step])
        act = (0.5 * upper * (1.0 + lax.erf(upper * 0.7071067811865476))).astype(BF16)
        acc_ref[...] += mm(act, wd_ref[at : at + step, :])
    return acc_ref[...].astype(BF16)


def weight_copies(block, sources, targets, sems):
    return [
        pltpu.make_async_copy(source.at[block], target, sems.at[n])
        for n, (source, target) in enumerate(zip(sources, targets))
    ]


def first_kernel(
    pattern, points, dest, gains, group, qkv_hbm, proj_hbm, up_hbm, down_hbm,
    out, chosen, q_ref, att_ref, acc_ref, wq, wp, wu, wd, sems, row_sems,
):
    copies = weight_copies(0, (qkv_hbm, proj_hbm, up_hbm, down_hbm), (wq, wp, wu, wd), sems)
    patches, picks = pattern.shape
    rows_here, channels = points.shape
    fetches = [
        pltpu.make_async_copy(
            group.at[pattern[p, j]],
            chosen.at[p, pl.ds((j + 1) * PATCH, PATCH)],
            row_sems.at[p * picks + j],
        )
        for p in range(patches)
        for j in range(picks)
    ]
    copies[0].start()
    for fetch in fetches:
        fetch.start()
    for copy in copies[1:]:
        copy.start()
    for p in range(patches):
        chosen[p, :PATCH] = points[p * PATCH : (p + 1) * PATCH]
    target = dest[...] >> 9
    devices = out.shape[0] // SLOTS
    on_device = lax.broadcasted_iota(jnp.int32, (devices, rows_here), 0) == target
    before = lax.broadcasted_iota(jnp.int32, (rows_here, rows_here), 0) < lax.broadcasted_iota(
        jnp.int32, (rows_here, rows_here), 1
    )
    earlier = mm(on_device.astype(BF16), before.astype(BF16))
    rank = jnp.sum(jnp.where(on_device, earlier, 0.0), axis=0, keepdims=True)
    slot = target * SLOTS + rank.astype(jnp.int32)
    gain = gains[0:1]
    copies[0].wait()
    q_ref[...] = mm(norm(points[...], gain), wq[:, :channels]).astype(BF16)
    for fetch in fetches:
        fetch.wait()

    def one(p, carry):
        hidden = norm(chosen[p], gain)
        kv = mm(hidden, wq[:, channels:]).astype(BF16)
        at = pl.multiple_of(p * PATCH, PATCH)
        att_ref[pl.ds(at, PATCH)] = attend_patch(
            q_ref[pl.ds(at, PATCH)], kv[:, :channels], kv[:, channels:]
        )
        return carry

    lax.fori_loop(0, patches, one, 0)
    done = finish(
        points[...], att_ref, gains[1:2], wp, wu, wd, acc_ref, [copy.wait for copy in copies[1:]]
    )
    step = 256
    for at in range(0, devices * SLOTS, step):
        match = lax.broadcasted_iota(jnp.int32, (step, rows_here), 0) + at == slot
        out[at : at + step] = mm(match.astype(BF16), done).astype(BF16)


def second_kernel(
    pattern, incoming, dest_all, gains, head, qkv_hbm, proj_hbm, up_hbm, down_hbm,
    features, normals, rows_ref, q_ref, kv_ref, att_ref, acc_ref, wq, wp, wu, wd, sems,
):
    copies = weight_copies(1, (qkv_hbm, proj_hbm, up_hbm, down_hbm), (wq, wp, wu, wd), sems)
    for copy in copies:
        copy.start()
    patches, picks = pattern.shape
    rows_here, channels = features.shape
    devices = dest_all.shape[0]
    slots = devices * SLOTS
    me = lax.axis_index("grp") * lax.axis_size("seq") + lax.axis_index("seq")
    dest = jnp.transpose(dest_all[...])
    mine = (dest >> 9) == me
    before = lax.broadcasted_iota(jnp.int32, (rows_here, rows_here), 0) > lax.broadcasted_iota(
        jnp.int32, (rows_here, rows_here), 1
    )
    rank = mm(before.astype(BF16), mine.astype(BF16)).astype(jnp.int32)
    place = jnp.where(mine, (dest & 511) + 1, 0)
    table = jnp.concatenate(
        [
            jnp.sum(jnp.where(rank == j, place, 0), axis=0, keepdims=True)
            for j in range(SLOTS)
        ],
        axis=0,
    )
    spread = (
        lax.broadcasted_iota(jnp.int32, (devices, slots), 1) // SLOTS
        == lax.broadcasted_iota(jnp.int32, (devices, slots), 0)
    ).astype(BF16)
    high = mm((table >> 4).astype(F32).astype(BF16), spread)
    low = mm((table & 15).astype(F32).astype(BF16), spread)
    of_rank = (
        lax.broadcasted_iota(jnp.int32, (SLOTS, slots), 1) % SLOTS
        == lax.broadcasted_iota(jnp.int32, (SLOTS, slots), 0)
    )
    slot_place = jnp.sum(
        jnp.where(of_rank, high * 16.0 + low, 0.0), axis=0, keepdims=True
    ).astype(jnp.int32)
    step = 256
    for at in range(0, rows_here, step):
        match = lax.broadcasted_iota(jnp.int32, (step, slots), 0) + (at + 1) == slot_place
        rows_ref[at : at + step] = mm(match.astype(BF16), incoming[...]).astype(BF16)
    copies[0].wait()
    hidden = norm(rows_ref[...], gains[2:3])
    q_ref[...] = mm(hidden, wq[:, :channels]).astype(BF16)
    kv_ref[...] = (
        mm(hidden, wq[:, channels:]).astype(BF16).reshape(patches, PATCH, 2 * channels)
    )

    def one(p, carry):
        kv = jnp.concatenate([kv_ref[p]] + [kv_ref[pattern[p, j]] for j in range(picks)], axis=0)
        at = pl.multiple_of(p * PATCH, PATCH)
        att_ref[pl.ds(at, PATCH)] = attend_patch(
            q_ref[pl.ds(at, PATCH)], kv[:, :channels], kv[:, channels:]
        )
        return carry

    lax.fori_loop(0, patches, one, 0)
    done = finish(
        rows_ref[...], att_ref, gains[3:4], wp, wu, wd, acc_ref, [copy.wait for copy in copies[1:]]
    )
    features[...] = done
    normals[...] = lax.dot_general(
        head[...], done, (((1,), (1,)), ((), ())), preferred_element_type=F32
    )


def shards(
    points, pattern_first, pattern_second, destination, norm_gains, w_qkv, w_proj, w_up, w_down, w_head
):
    rows_here, channels = points.shape
    patches = rows_here // PATCH
    ff = w_up.shape[2]
    devices = lax.axis_size("grp") * lax.axis_size("seq")
    slots = devices * SLOTS
    vmem = pl.BlockSpec(memory_space=pltpu.VMEM)
    smem = pl.BlockSpec(memory_space=pltpu.SMEM)
    anywhere = pl.BlockSpec(memory_space=pl.ANY)
    weights = [
        pltpu.VMEM((channels, 3 * channels), BF16),
        pltpu.VMEM((channels, channels), BF16),
        pltpu.VMEM((channels, ff), BF16),
        pltpu.VMEM((ff, channels), BF16),
        pltpu.SemaphoreType.DMA((4,)),
    ]
    params = pltpu.CompilerParams(vmem_limit_bytes=48 << 20)
    work = 2 * rows_here * channels * (4 * channels + 2 * ff)
    cost = pl.CostEstimate(flops=2 * work, bytes_accessed=8 << 20, transcendentals=rows_here * ff)
    group = lax.all_gather(points, "seq", axis=0, tiled=True).reshape(-1, PATCH, channels)
    dest_row = destination.reshape(1, rows_here)
    dest_all = lax.all_gather(dest_row, ("grp", "seq"), axis=0, tiled=True)
    outgoing = pl.pallas_call(
        first_kernel,
        out_shape=jax.ShapeDtypeStruct((slots, channels), BF16),
        in_specs=[smem, vmem, vmem, vmem] + [anywhere] * 5,
        out_specs=vmem,
        scratch_shapes=[
            pltpu.VMEM((patches, 4 * PATCH, channels), BF16),
            pltpu.VMEM((rows_here, channels), BF16),
            pltpu.VMEM((rows_here, channels), BF16),
            pltpu.VMEM((rows_here, channels), F32),
        ]
        + weights
        + [pltpu.SemaphoreType.DMA((patches * pattern_first.shape[1],))],
        compiler_params=params,
        cost_estimate=cost,
        name="first_block",
    )(pattern_first, points, dest_row, norm_gains, group, w_qkv, w_proj, w_up, w_down)
    incoming = lax.all_to_all(
        outgoing.reshape(devices, SLOTS, channels), ("grp", "seq"), split_axis=0, concat_axis=0, tiled=True
    ).reshape(slots, channels)
    features, normals = pl.pallas_call(
        second_kernel,
        out_shape=(
            jax.ShapeDtypeStruct((rows_here, channels), BF16),
            jax.ShapeDtypeStruct((w_head.shape[0], rows_here), F32),
        ),
        in_specs=[smem, vmem, vmem, vmem, vmem] + [anywhere] * 4,
        out_specs=(vmem, vmem),
        scratch_shapes=[
            pltpu.VMEM((rows_here, channels), BF16),
            pltpu.VMEM((rows_here, channels), BF16),
            pltpu.VMEM((patches, PATCH, 2 * channels), BF16),
            pltpu.VMEM((rows_here, channels), BF16),
            pltpu.VMEM((rows_here, channels), F32),
        ]
        + weights,
        compiler_params=params,
        cost_estimate=cost,
        name="second_block",
    )(pattern_second, incoming, dest_all, norm_gains, w_head, w_qkv, w_proj, w_up, w_down)
    return features, normals


def solution(mesh):
    split = P(("grp", "seq"))
    return jax.shard_map(
        shards,
        mesh=mesh,
        in_specs=(split, split, split, split) + (P(),) * 6,
        out_specs=(split, P(None, ("grp", "seq"))),
        check_vma=False,
    )
```

time: 323 us -> 181 us (0.56); the launches traced: 319 us -> 181 us
  matrix products: 71 us -> 0 us
  waiting for transfers between devices: 138 us -> 78.6 us
  local copies, waits for them, and re-layouts: 64.3 us -> 7.63 us
  blocking collectives: 0 us -> 43.4 us
  Pallas kernels: 0 us -> 29.1 us
  starting transfers between devices: 19.1 us -> 7.76 us
  other arithmetic: 11 us -> 0 us
    dot_general x11 -> x0, matrix products: 71 us -> none  [the longest x2 27.3 us: finish(): jnp.dot(act, w_down[section], preferred_element_type=jnp.float32)]
    all_gather x0 -> x1, blocking collectives: none -> 43.4 us  [shards(): dest_all = lax.all_gather(dest_row, ('grp', 'seq'), axis=0, tiled=True)]
    all_gather x2 -> x1, waiting for transfers between devices: 121 us -> 77.9 us  [shards(): lax.all_gather(points, 'seq', axis=0, tiled=True)]
    gather x8 -> x0, local copies, waits for them, and re-layouts: 33.1 us -> none  [the longest x1 7.62 us: shards(): key_chosen = key_group.reshape(-1, PATCH, channels)[pattern_first]]
    pallas_call x0 -> x2, Pallas kernels: none -> 29.1 us  [the longest x1 15.1 us: shards(): pl.pallas_call(first_kernel, out_shape=jax.ShapeDtypeStruct((slots, chann...]
    all_to_all x2 -> x1, waiting for transfers between devices: 17.2 us -> 0.01 us  [shards(): lax.all_to_all(outgoing.reshape(devices, SLOTS, channels), ('grp', 'seq')...]
    another operation x7 -> x0, local copies, waits for them, and re-layouts: 14.6 us -> none  [the longest x2 7.29 us: attend(): vh = value_rows.reshape(count, -1, HEADS, head_dim)]
    all_to_all x2 -> x1, starting transfers between devices: 19 us -> 7.73 us  [shards(): lax.all_to_all(outgoing.reshape(devices, SLOTS, channels), ('grp', 'seq')...]
  transfers between devices with their start and end apart: 4 -> 2, of which waited for: 3 -> 1; matrix products, arithmetic and copies ran while one was open for 24% -> 0% of each run, Pallas kernels for 0% -> 0%
where the time goes in v1:
time: 181 us
  waiting for transfers between devices  78.6 us (43%)
  blocking collectives  43.4 us (24%)
  Pallas kernels  29.1 us (16%)
  between operations  14.1 us (8%)
  starting transfers between devices  7.76 us (4%)
  local copies, waits for them, and re-layouts  7.63 us (4%)
    all_gather x1, waiting for transfers between devices, shards(): lax.all_gather(points, 'seq', axis=0, tiled=True)  77.9 us
    all_gather x1, blocking collectives, shards(): dest_all = lax.all_gather(dest_row, ('grp', 'seq'), axis=0, tiled=True)  43.4 us
    pallas_call x1, Pallas kernels, shards(): pl.pallas_call(first_kernel, out_shape=jax.ShapeDtypeStruct((slots, chann...  15.1 us
    pallas_call x1, Pallas kernels, shards(): pl.pallas_call(second_kernel, out_shape=(jax.ShapeDtypeStruct((rows_here,...  14 us
    all_to_all x1, starting transfers between devices, shards(): lax.all_to_all(outgoing.reshape(devices, SLOTS, channels), ('grp', 'seq')...  7.73 us
    unnamed x25, local copies, waits for them, and re-layouts  7.63 us
  transfers between devices with their start and end apart: 2, of which 1 were waited for; matrix products, arithmetic and copies ran while one was open for 0% of the time, Pallas kernels for 0%

profile of v1, /device:TPU:1, one launch (start us, length us, event | category | flops | bytes accessed | tf_op | source)
XLA Modules:
  0.0 180.6 jit_solution(5067238812486572558)
XLA Ops:
  7.2 0.0 all-gather.4.cloned.1.call-start
  7.2 0.7 all-gather.4.cloned.1.call-update
  7.9 0.8 copy.14.pattern
  8.7 77.9 %all-gather.4.cloned.1.call-done = bf16[16384,512]{1,0:T(8,128)(2,1)} async-done(((bf16[512,512]{1,0:T(8,128)(2,1)}), bf16[16384,512]{1,0:T(8,128)(2,1)}) %all-gather.4.cloned.1.call-update) | async-done | bytes 16777232 | tf_op jit(solution)/shard_map/all_gather | solution.py:222
  86.5 0.0 copy-start
  86.5 1.9 %copy-done = bf16[2,512,1536]{2,1,0:T(8,128)(2,1)S(1)} copy-done((bf16[2,512,1536]{2,1,0:T(8,128)(2,1)S(1)}, bf16[2,512,1536]{2,1,0:T(8,128)(2,1)}, u32[]{:S(2)}) %copy-start) | copy-done | bytes 3145752
  88.4 0.0 copy-start.2
  88.4 1.0 copy-done.2
  89.5 0.0 copy-start.3
  89.5 1.2 copy-done.3
  90.7 0.0 copy-start.5
  90.7 0.7 copy-done.5
  91.4 0.0 copy-start.7
  91.4 0.7 copy-done.7
  92.1 0.0 copy-start.10
  92.1 0.0 copy-start.8
  92.1 0.0 copy-start.1
  92.1 0.0 copy-start.6
  92.1 0.0 copy-start.9
  92.1 15.1 %first_block.1 = bf16[1024,512]{1,0:T(8,128)(2,1)} custom-call(s32[8,3]{1,0:T(8,128)S(1)} %copy.14.pattern, bf16[512,512]{1,0:T(8,128)(2,1)S(1)} %copy-done.2, s32[1,512]{1,0:T(1,128)S(1)} %bitcast.9, f32[4,512]{1,0:T(4,128)S(1)} %copy-done.5, bf16[256,64,512]{2,1,0:T(8,128)(2,1)} %bitcast.11, bf16[2,512,1536]{2,1,0:T(8,128)(2,1)S(1)} %copy-done, ...), custom_call_target="tpu_custom_call" | custom-call | flops 6442450944 | bytes 8388608 | tf_op jit(solution)/shard_map/first_block/pallas_call | solution.py:225
  107.2 7.7 %all-to-all-start = ((bf16[128,8,512]{2,1,0:T(8,128)(2,1)}), bf16[128,8,512]{2,1,0:T(8,128)(2,1)}, u32[]{:S(2)}, u32[]{:S(2)}) async-start(bf16[128,8,512]{2,1,0:T(8,128)(2,1)} %bitcast.2), calls=%async_computation | async-start | bytes 2097152 | tf_op jit(solution)/shard_map/all_to_all | solution.py:242
  114.9 0.0 copy-done.10
  114.9 0.1 copy.15.pattern
  115.0 0.0 copy-done.8
  115.0 43.4 %all-gather.1 = s32[128,1,512]{2,1,0:T(1,128)S(1)} all-gather(s32[1,1,512]{2,1,0:T(1,128)S(1)} %bitcast.10), channel_id=2, replica_groups=mesh['grp'=4,'seq'=32] {'grp','seq'}, dimensions={0}, use_global_device_ids=true | all-gather | bytes 264192 | tf_op jit(solution)/shard_map/all_gather | solution.py:224
  158.4 0.0 all-to-all-done
  158.5 0.0 copy-done.1
  158.5 0.0 copy-done.6
  158.5 0.0 copy-done.9
  158.5 0.0 copy-start.4
  158.5 1.2 copy-done.4
  159.7 14.0 %second_block.1 = (bf16[512,512]{1,0:T(8,128)(2,1)}, f32[3,512]{1,0:T(4,128)}) custom-call(s32[8,3]{1,0:T(8,128)S(1)} %copy.15.pattern, bf16[1024,512]{1,0:T(8,128)(2,1)} %bitcast.3.incoming, s32[128,512]{1,0:T(8,128)S(1)} %bitcast.8, f32[4,512]{1,0:T(4,128)S(1)} %copy-done.6, bf16[3,512]{1,0:T(4,128)(2,1)S(1)} %copy-done.9, ...), custom_call_target="tpu_custom_call" | custom-call | flops 6442450944 | bytes 8388608 | tf_op jit(solution)/shard_map/second_block/pallas_call | solution.py:245
  (1 shorter events, 0.0 us)
Async XLA Ops:
  7.2 79.4 %all-gather.4.cloned.1.call-start = ((), (), s32[]{:S(2)}) async-start(), calls=%async_computation.1 | async-start | bytes 17301504 | tf_op jit(solution)/shard_map/all_gather | solution.py:222
  86.5 1.9 %copy-start = (bf16[2,512,1536]{2,1,0:T(8,128)(2,1)S(1)}, bf16[2,512,1536]{2,1,0:T(8,128)(2,1)}, u32[]{:S(2)}) copy-start(bf16[2,512,1536]{2,1,0:T(8,128)(2,1)} %qkv_hbm.3) | copy-start | bytes 9437188
  88.4 1.0 copy-start.2
  89.5 1.2 copy-start.3
  90.7 0.7 copy-start.5
  91.4 0.7 copy-start.7
  92.1 22.9 %copy-start.10 = (s32[8,3]{0,1:T(4,128)S(1)}, s32[8,3]{0,1:T(4,128)}, u32[]{:S(2)}) copy-start(s32[8,3]{0,1:T(4,128)} %param.12) | copy-start | bytes 292
  92.1 23.0 %copy-start.8 = (s32[512]{0:T(512)S(1)}, s32[512]{0:T(512)}, u32[]{:S(2)}) copy-start(s32[512]{0:T(512)} %param.13) | copy-start | bytes 6148
  92.1 66.4 %copy-start.1 = (bf16[2,512,1536]{2,1,0:T(8,128)(2,1)S(1)}, bf16[2,512,1536]{2,1,0:T(8,128)(2,1)}, u32[]{:S(2)}) copy-start(bf16[2,512,1536]{2,1,0:T(8,128)(2,1)} %qkv_hbm.3) | copy-start | bytes 9437188
  92.1 66.4 %copy-start.6 = (f32[4,512]{1,0:T(4,128)S(1)}, f32[4,512]{1,0:T(4,128)}, u32[]{:S(2)}) copy-start(f32[4,512]{1,0:T(4,128)} %gains.3) | copy-start | bytes 24580
  92.1 66.4 %copy-start.9 = (bf16[3,512]{1,0:T(4,128)(2,1)S(1)}, bf16[3,512]{1,0:T(4,128)(2,1)}, u32[]{:S(2)}) copy-start(bf16[3,512]{1,0:T(4,128)(2,1)} %head.1) | copy-start | bytes 9220
  107.2 51.3 %all-to-all-start = ((bf16[128,8,512]{2,1,0:T(8,128)(2,1)}), bf16[128,8,512]{2,1,0:T(8,128)(2,1)}, u32[]{:S(2)}, u32[]{:S(2)}) async-start(bf16[128,8,512]{2,1,0:T(8,128)(2,1)} %bitcast.2), calls=%async_computation | async-start | bytes 2097152 | tf_op jit(solution)/shard_map/all_to_all | solution.py:242
  158.5 1.2 copy-start.4
Sparse Core Ops, SparseCore 0:
  10.3 76.2 all-gather.3

commit v2 on v1

v2 whole, which is shorter than its diff:
```python
import functools

import jax
import jax.numpy as jnp
from jax import lax
from jax.experimental import pallas as pl
from jax.experimental.pallas import tpu as pltpu
from jax.sharding import PartitionSpec as P

HEADS = 8
PATCH = 64
SLOTS = 8
GROUP_HEADS = 4
BF16 = jnp.bfloat16
F32 = jnp.float32
SIDE = 4
REQUESTS = 2
MESH = pl.DeviceIdType.MESH


def norm(rows, gains):
    values = rows.astype(F32)
    centered = values - jnp.mean(values, axis=-1, keepdims=True)
    spread = jnp.mean(centered * centered, axis=-1, keepdims=True)
    return (centered * lax.rsqrt(spread + 1e-05) * gains).astype(BF16)


def mm(a, b):
    return jnp.dot(a, b, preferred_element_type=F32)


def attend_patch(queries, keys, values):
    width = GROUP_HEADS * PATCH
    lane = lax.broadcasted_iota(jnp.int32, (PATCH, width), 1) // PATCH
    mixed = []
    for part in range(HEADS // GROUP_HEADS):
        cols = slice(part * width, (part + 1) * width)
        q = queries[:, cols]
        spread = jnp.concatenate(
            [jnp.where(lane == head, q, jnp.zeros_like(q)) for head in range(GROUP_HEADS)], axis=0
        )
        scores = lax.dot_general(
            spread, keys[:, cols], (((1,), (1,)), ((), ())), preferred_element_type=F32
        )
        top = jnp.max(scores, axis=-1, keepdims=True)
        weights = jnp.exp((scores - top) * PATCH ** (-0.5))
        total = jnp.sum(weights, axis=-1, keepdims=True)
        out = mm(weights.astype(BF16), values[:, cols]) * (1.0 / total)
        acc = jnp.where(lane == 0, out[:PATCH], 0.0)
        for head in range(1, GROUP_HEADS):
            acc = acc + jnp.where(lane == head, out[head * PATCH : (head + 1) * PATCH], 0.0)
        mixed.append(acc)
    return jnp.concatenate(mixed, axis=1).astype(BF16)


def finish(rows, att_ref, gains, wp_ref, wu_ref, wd_ref, acc_ref, waits):
    waits[0]()
    first = (rows.astype(F32) + mm(att_ref[...], wp_ref[...])).astype(BF16)
    hidden = norm(first, gains)
    acc_ref[...] = first.astype(F32)
    waits[1]()
    waits[2]()
    ff = wu_ref.shape[1]
    step = 512
    for at in range(0, ff, step):
        upper = mm(hidden, wu_ref[:, at : at + step])
        act = (0.5 * upper * (1.0 + lax.erf(upper * 0.7071067811865476))).astype(BF16)
        acc_ref[...] += mm(act, wd_ref[at : at + step, :])
    return acc_ref[...].astype(BF16)


def weight_copies(block, sources, targets, sems):
    return [
        pltpu.make_async_copy(source.at[block], target, sems.at[n])
        for n, (source, target) in enumerate(zip(sources, targets))
    ]


def first_kernel(
    pattern, points_hbm, dest_hbm, gains_hbm, qkv_hbm, proj_hbm, up_hbm, down_hbm,
    incoming, in_places, points, dest, gains, asks, out_places, hx0, hx1, hx2, hx3, hz0, hz1, hz2, hz3, got_x, got_z, pats, send, table, picks,
    chosen, q_ref, att_ref, acc_ref, outgoing, wq, wp, wu, wd, weight_sems,
    pat_sems, step_sems, send_sems, recv_sems, table_sem, ready_plane, ready_all, load_sems, row_sems, place_sems,
):
    grp = lax.axis_index("grp")
    seq = lax.axis_index("seq")
    x, z, c = seq // (2 * SIDE), (seq // 2) % SIDE, seq % 2
    patches, patch, channels = points.shape
    half = channels // 2
    places = 2 * SIDE
    loads = [
        pltpu.make_async_copy(source, target, load_sems.at[n])
        for n, (source, target) in enumerate(((points_hbm, points), (dest_hbm, dest), (gains_hbm, gains)))
    ]
    copies = weight_copies(0, (qkv_hbm, proj_hbm, up_hbm, down_hbm), (wq, wp, wu, wd), weight_sems)
    for copy in loads + copies:
        copy.start()
    lane = lax.broadcasted_iota(jnp.int32, asks.shape, 1)
    asking = jnp.full(asks.shape, -1, jnp.int32)
    named = [pattern[j, p] for p in range(patches) for j in range(pattern.shape[0])]
    for n, name in enumerate(named):
        asking = jnp.where(lane == n, name, asking)
    asks[...] = asking

    def at(axis, step, other):
        core = (c + other) % 2
        if axis == 0:
            place = (x + step) % SIDE
            return (grp, (place * SIDE + z) * 2 + core), place * 2 + core
        place = (z + step) % SIDE
        return (grp, (x * SIDE + place) * 2 + core), place * 2 + core

    def across(step):
        return ((grp + step) % SIDE, seq)

    peers = [(axis, step, other) for axis in (0, 1) for step in range(SIDE) for other in (0, 1)]
    peers = [peer for peer in peers if peer[1:] != (0, 0)]
    steps = (1, SIDE - 1, 2)
    barrier = pltpu.get_barrier_semaphore()
    for peer in peers:
        pl.semaphore_signal(barrier, inc=1, device_id=at(*peer)[0], device_id_type=MESH)
    for step in steps:
        pl.semaphore_signal(barrier, inc=1, device_id=across(step), device_id_type=MESH)
    pl.semaphore_wait(barrier, len(peers) + len(steps))

    along = (x, z)
    mine = (x * 2 + c, z * 2 + c)
    held = ((hx0, hx1, hx2, hx3), (hz0, hz1, hz2, hz3))
    got = (got_x, got_z)

    def first_step(axis, step):
        return pltpu.make_async_remote_copy(
            src_ref=points.at[:, :, pl.ds(axis * half, half)],
            dst_ref=held[axis][SIDE - step],
            send_sem=step_sems.at[axis, 0, step],
            recv_sem=step_sems.at[axis, 1, SIDE - step],
            device_id=at(axis, step, 0)[0],
            device_id_type=MESH,
        )

    def ask(axis, step, other, place):
        return pltpu.make_async_remote_copy(
            src_ref=asks,
            dst_ref=pats.at[axis * places + place],
            send_sem=pat_sems.at[0, axis * places + step * 2 + other],
            recv_sem=pat_sems.at[1, axis * places + place],
            device_id=at(axis, step, other)[0],
            device_id_type=MESH,
        )

    for peer in peers:
        ask(*peer, mine[peer[0]]).start()
    loads[0].wait()
    for step in steps:
        for axis in (0, 1):
            first_step(axis, step).start()
    for step in steps:
        pl.semaphore_signal(ready_plane, inc=1, device_id=at(0, step, 0)[0], device_id_type=MESH)
    for axis in (0, 1):
        held[axis][0][...] = points[:, :, axis * half : (axis + 1) * half]
        pats[axis * places + mine[axis]] = asks[...]
    for peer in peers:
        ask(*peer, at(*peer)[1]).wait()

    asked = pats[...].reshape(2 * places, pats.shape[2])
    lane = lax.broadcasted_iota(jnp.int32, asked.shape, 1)
    in_row = lax.broadcasted_iota(jnp.int32, asked.shape, 0) < places
    found = jnp.zeros_like(asked)
    for k in range(SIDE):
        source = jnp.where(in_row, (x * SIDE + k) * 2 + c, (k * SIDE + z) * 2 + c)
        match = (asked >> 3) == source
        first = jnp.min(jnp.where(match, lane, asked.shape[1]), axis=1, keepdims=True)
        local = asked & 7
        one = jnp.sum(jnp.where(match & (lane == first), local, 0), axis=1, keepdims=True)
        two = jnp.sum(jnp.where(match & (lane != first), local, 0), axis=1, keepdims=True) & 7
        found = jnp.where(lane == 2 * k, one, jnp.where(lane == 2 * k + 1, two, found))
    table[...] = found
    load = pltpu.make_async_copy(table, picks, table_sem)
    load.start()
    load.wait()

    def pass_on(axis, step, other, turn, k, place):
        return pltpu.make_async_remote_copy(
            src_ref=send.at[axis, step * 2 + other, turn],
            dst_ref=got[axis].at[place, k],
            send_sem=send_sems.at[axis, step * 2 + other, turn],
            recv_sem=recv_sems.at[axis, place, k],
            device_id=at(1 - axis, step, other)[0],
            device_id_type=MESH,
        )

    askers = [(step, other) for step in steps + (0,) for other in (0, 1)]
    for turn in (0,) + tuple(SIDE - step for step in steps):
        for axis in (0, 1):
            k = (along[axis] + turn) % SIDE
            if turn:
                first_step(axis, SIDE - turn).wait_recv()
            for step, other in askers:
                row = (1 - axis) * places + at(1 - axis, step, other)[1]
                for r in range(REQUESTS):
                    part = held[axis][turn][picks[row, REQUESTS * k + r]]
                    if (step, other) == (0, 0):
                        got[axis][mine[1 - axis], k, r] = part
                    else:
                        send[axis, step * 2 + other, turn, r] = part
                if (step, other) != (0, 0):
                    pass_on(axis, step, other, turn, k, mine[1 - axis]).start()
    pl.semaphore_wait(ready_plane, len(steps))
    for step in steps:
        pl.semaphore_signal(ready_all, inc=1, device_id=across(step), device_id_type=MESH)

    rows_here = patches * patch
    devices = incoming.shape[0]
    loads[1].wait()
    loads[2].wait()
    target = dest[...] >> 9
    on_device = lax.broadcasted_iota(jnp.int32, (devices, rows_here), 0) == target
    before = lax.broadcasted_iota(jnp.int32, (rows_here, rows_here), 0) < lax.broadcasted_iota(
        jnp.int32, (rows_here, rows_here), 1
    )
    earlier = mm(on_device.astype(BF16), before.astype(BF16))
    rank = jnp.sum(jnp.where(on_device, earlier, 0.0), axis=0, keepdims=True)
    slot = target * SLOTS + rank.astype(jnp.int32)
    lane = lax.broadcasted_iota(jnp.int32, (devices, 128), 1)
    place = (dest[...] & 511) + 1
    table_out = jnp.zeros((devices, 128), jnp.int32)
    for j in range(SLOTS):
        here = jnp.where(on_device & (earlier == j), place, 0)
        table_out = jnp.where(lane == j, jnp.sum(here, axis=1, keepdims=True), table_out)
    out_places[...] = table_out.reshape(devices, 1, 128)

    pl.semaphore_wait(ready_all, len(steps))
    group = devices // SIDE
    me = grp * group + seq

    def send_to(source, target, sems, to):
        return pltpu.make_async_remote_copy(
            src_ref=source.at[to],
            dst_ref=target.at[me],
            send_sem=sems.at[0],
            recv_sem=sems.at[1],
            device_id=(to // group, to % group),
            device_id_type=MESH,
        )

    def arrive(source, target, sems):
        blocks = pl.ds(0, devices - 1)
        pltpu.make_async_remote_copy(
            src_ref=source.at[blocks],
            dst_ref=target.at[blocks],
            send_sem=sems.at[0],
            recv_sem=sems.at[1],
            device_id=across(1),
            device_id_type=MESH,
        ).wait()

    def send_places(k, carry):
        send_to(out_places, in_places, place_sems, (me + k) % devices).start()
        return carry

    lax.fori_loop(1, devices, send_places, 0)
    in_places[me] = out_places[me]
    gain = gains[0:1]
    rows = points[...].reshape(rows_here, channels)
    copies[0].wait()
    q_ref[...] = mm(norm(rows, gain), wq[:, :channels]).astype(BF16)

    for axis in (0, 1):
        for step in steps:
            first_step(axis, step).wait_send()
        for step, other in askers:
            if (step, other) != (0, 0):
                for k in range(SIDE):
                    pass_on(axis, step, other, k, k, at(1 - axis, step, other)[1]).wait()

    owners = []
    for p in range(patches):
        chosen[p, :patch] = points[p]
        for j in range(pattern.shape[0]):
            owner = named[p * pattern.shape[0] + j] >> 3
            r = jnp.int32(0)
            for earlier_owner in owners:
                r = r + jnp.where(earlier_owner == owner, 1, 0)
            owners.append(owner)
            r = jnp.minimum(r, REQUESTS - 1)
            ox, oz, oc = owner // places, (owner // 2) % SIDE, owner % 2
            to = slice((j + 1) * patch, (j + 2) * patch)
            chosen[p, to, :half] = got_x[oz * 2 + oc, ox, r]
            chosen[p, to, half:] = got_z[ox * 2 + oc, oz, r]

    def one(p, carry):
        hidden = norm(chosen[p], gain)
        kv = mm(hidden, wq[:, channels:]).astype(BF16)
        start = pl.multiple_of(p * patch, patch)
        att_ref[pl.ds(start, patch)] = attend_patch(
            q_ref[pl.ds(start, patch)], kv[:, :channels], kv[:, channels:]
        )
        return carry

    lax.fori_loop(0, patches, one, 0)
    done = finish(rows, att_ref, gains[1:2], wp, wu, wd, acc_ref, [copy.wait for copy in copies[1:]])

    for turn in range(SIDE):
        to_grp = (grp + turn) % SIDE
        match = (
            lax.broadcasted_iota(jnp.int32, (group * SLOTS, rows_here), 0) + to_grp * (group * SLOTS) == slot
        )
        outgoing[pl.ds(to_grp * group, group)] = (
            mm(match.astype(BF16), done).astype(BF16).reshape(group, SLOTS, channels)
        )

        def send_rows(k, carry):
            send_to(outgoing, incoming, row_sems, to_grp * group + (seq + k) % group).start()
            return carry

        lax.fori_loop(1 if turn == 0 else 0, group, send_rows, 0)
    incoming[me] = outgoing[me]
    arrive(out_places, in_places, place_sems)
    arrive(outgoing, incoming, row_sems)


def second_kernel(
    pattern, incoming, places, gains_hbm, head_hbm, qkv_hbm, proj_hbm, up_hbm, down_hbm,
    features, normals, gains, head, rows_ref, q_ref, kv_ref, att_ref, acc_ref, wq, wp, wu, wd, sems, load_sems,
):
    loads = [
        pltpu.make_async_copy(source, target, load_sems.at[n])
        for n, (source, target) in enumerate(
            ((gains_hbm, gains), (head_hbm, head))
        )
    ]
    copies = weight_copies(1, (qkv_hbm, proj_hbm, up_hbm, down_hbm), (wq, wp, wu, wd), sems)
    for copy in loads + copies:
        copy.start()
    picks, patches = pattern.shape
    rows_here, channels = features.shape
    devices = places.shape[0]
    slots = devices * SLOTS
    table = jnp.transpose(places[...].reshape(devices, 128))[:SLOTS]
    spread = (
        lax.broadcasted_iota(jnp.int32, (devices, slots), 1) // SLOTS
        == lax.broadcasted_iota(jnp.int32, (devices, slots), 0)
    ).astype(BF16)
    high = mm((table >> 4).astype(F32).astype(BF16), spread)
    low = mm((table & 15).astype(F32).astype(BF16), spread)
    of_rank = (
        lax.broadcasted_iota(jnp.int32, (SLOTS, slots), 1) % SLOTS
        == lax.broadcasted_iota(jnp.int32, (SLOTS, slots), 0)
    )
    slot_place = jnp.sum(
        jnp.where(of_rank, high * 16.0 + low, 0.0), axis=0, keepdims=True
    ).astype(jnp.int32)
    step = 256
    for at in range(0, rows_here, step):
        match = lax.broadcasted_iota(jnp.int32, (step, slots), 0) + (at + 1) == slot_place
        rows_ref[at : at + step] = mm(match.astype(BF16), incoming[...]).astype(BF16)
    loads[0].wait()
    copies[0].wait()
    hidden = norm(rows_ref[...], gains[2:3])
    q_ref[...] = mm(hidden, wq[:, :channels]).astype(BF16)
    kv_ref[...] = (
        mm(hidden, wq[:, channels:]).astype(BF16).reshape(patches, PATCH, 2 * channels)
    )

    def one(p, carry):
        kv = jnp.concatenate([kv_ref[p]] + [kv_ref[pattern[j, p]] for j in range(picks)], axis=0)
        at = pl.multiple_of(p * PATCH, PATCH)
        att_ref[pl.ds(at, PATCH)] = attend_patch(
            q_ref[pl.ds(at, PATCH)], kv[:, :channels], kv[:, channels:]
        )
        return carry

    lax.fori_loop(0, patches, one, 0)
    done = finish(
        rows_ref[...], att_ref, gains[3:4], wp, wu, wd, acc_ref, [copy.wait for copy in copies[1:]]
    )
    features[...] = done
    loads[1].wait()
    normals[...] = lax.dot_general(
        head[...], done, (((1,), (1,)), ((), ())), preferred_element_type=F32
    )


def shards(
    points, pattern_first, pattern_second, destination, norm_gains, w_qkv, w_proj, w_up, w_down, w_head
):
    rows_here, channels = points.shape
    patches = rows_here // PATCH
    ff = w_up.shape[2]
    devices = lax.axis_size("grp") * lax.axis_size("seq")
    slots = devices * SLOTS
    vmem = pl.BlockSpec(memory_space=pltpu.VMEM)
    smem = pl.BlockSpec(memory_space=pltpu.SMEM)
    hbm = pl.BlockSpec(memory_space=pltpu.HBM)
    weights = [
        pltpu.VMEM((channels, 3 * channels), BF16),
        pltpu.VMEM((channels, channels), BF16),
        pltpu.VMEM((channels, ff), BF16),
        pltpu.VMEM((ff, channels), BF16),
        pltpu.SemaphoreType.DMA((4,)),
    ]
    params = pltpu.CompilerParams(vmem_limit_bytes=48 << 20)
    work = 2 * rows_here * channels * (4 * channels + 2 * ff)
    cost = pl.CostEstimate(flops=2 * work, bytes_accessed=8 << 20, transcendentals=rows_here * ff)
    places = 2 * SIDE
    half = channels // 2
    keep = lambda array: pltpu.with_memory_space_constraint(array, pltpu.HBM)
    stacks = [keep(array) for array in (w_qkv, w_proj, w_up, w_down)]
    incoming, places_in = pl.pallas_call(
        first_kernel,
        out_shape=(
            jax.ShapeDtypeStruct((devices, SLOTS, channels), BF16),
            jax.ShapeDtypeStruct((devices, 1, 128), jnp.int32),
        ),
        in_specs=[smem] + [hbm] * 7,
        out_specs=(vmem, vmem),
        scratch_shapes=[
            pltpu.VMEM((patches, PATCH, channels), BF16),
            pltpu.VMEM((1, rows_here), jnp.int32),
            pltpu.VMEM(norm_gains.shape, F32),
            pltpu.VMEM((1, 128), jnp.int32),
            pltpu.VMEM((devices, 1, 128), jnp.int32),
        ]
        + [pltpu.VMEM((patches, PATCH, half), BF16)] * (2 * SIDE)
        + [pltpu.VMEM((places, SIDE, REQUESTS, PATCH, half), BF16)] * 2
        + [
            pltpu.VMEM((2 * places, 1, 128), jnp.int32),
            pltpu.VMEM((2, places, SIDE, REQUESTS, PATCH, half), BF16),
            pltpu.VMEM((2 * places, 128), jnp.int32),
            pltpu.SMEM((2 * places, 128), jnp.int32),
            pltpu.VMEM((patches, 4 * PATCH, channels), BF16),
            pltpu.VMEM((rows_here, channels), BF16),
            pltpu.VMEM((rows_here, channels), BF16),
            pltpu.VMEM((rows_here, channels), F32),
            pltpu.VMEM((devices, SLOTS, channels), BF16),
        ]
        + weights
        + [
            pltpu.SemaphoreType.DMA((2, 2 * places)),
            pltpu.SemaphoreType.DMA((2, 2, SIDE)),
            pltpu.SemaphoreType.DMA((2, places, SIDE)),
            pltpu.SemaphoreType.DMA((2, places, SIDE)),
            pltpu.SemaphoreType.DMA,
            pltpu.SemaphoreType.REGULAR,
            pltpu.SemaphoreType.REGULAR,
            pltpu.SemaphoreType.DMA((3,)),
            pltpu.SemaphoreType.DMA((2,)),
            pltpu.SemaphoreType.DMA((2,)),
        ],
        compiler_params=pltpu.CompilerParams(
            vmem_limit_bytes=48 << 20, collective_id=0, has_side_effects=True
        ),
        cost_estimate=cost,
        name="first_block",
    )(
        pattern_first.T,
        keep(points.reshape(patches, PATCH, channels)),
        keep(destination.reshape(1, rows_here)),
        keep(norm_gains),
        *stacks,
    )
    features, normals = pl.pallas_call(
        second_kernel,
        out_shape=(
            jax.ShapeDtypeStruct((rows_here, channels), BF16),
            jax.ShapeDtypeStruct((w_head.shape[0], rows_here), F32),
        ),
        in_specs=[smem, vmem, vmem] + [hbm] * 6,
        out_specs=(vmem, vmem),
        scratch_shapes=[
            pltpu.VMEM(norm_gains.shape, F32),
            pltpu.VMEM(w_head.shape, BF16),
            pltpu.VMEM((rows_here, channels), BF16),
            pltpu.VMEM((rows_here, channels), BF16),
            pltpu.VMEM((patches, PATCH, 2 * channels), BF16),
            pltpu.VMEM((rows_here, channels), BF16),
            pltpu.VMEM((rows_here, channels), F32),
        ]
        + weights
        + [pltpu.SemaphoreType.DMA((2,))],
        compiler_params=params,
        cost_estimate=cost,
        name="second_block",
    )(
        pattern_second.T,
        incoming.reshape(slots, channels),
        places_in,
        keep(norm_gains),
        keep(w_head),
        *stacks,
    )
    return features, normals


def solution(mesh):
    split = P(("grp", "seq"))
    return jax.shard_map(
        shards,
        mesh=mesh,
        in_specs=(split, split, split, split) + (P(),) * 6,
        out_specs=(split, P(None, ("grp", "seq"))),
        check_vma=False,
    )
```

time: 181 us -> 89.8 us (0.50)
  waiting for transfers between devices: 78.6 us -> 0 us
  Pallas kernels: 29.1 us -> 88.1 us
  blocking collectives: 43.4 us -> 0 us
  between operations: 14.1 us -> 0.66 us
  starting transfers between devices: 7.76 us -> 0 us
  local copies, waits for them, and re-layouts: 7.63 us -> 0.68 us
    all_gather x1 -> x0, waiting for transfers between devices: 77.9 us -> none  [shards(): lax.all_gather(points, 'seq', axis=0, tiled=True)]
    pallas_call x1, Pallas kernels: 15.1 us -> 74.9 us  [shards(): pl.pallas_call(first_kernel, out_shape=(jax.ShapeDtypeStruct((devices, SL...]
    all_gather x1 -> x0, blocking collectives: 43.4 us -> none  [shards(): dest_all = lax.all_gather(dest_row, ('grp', 'seq'), axis=0, tiled=True)]
    all_to_all x1 -> x0, starting transfers between devices: 7.73 us -> none  [shards(): lax.all_to_all(outgoing.reshape(devices, SLOTS, channels), ('grp', 'seq')...]
    unnamed x25 -> x4, local copies, waits for them, and re-layouts: 7.63 us -> 0.68 us
  transfers between devices with their start and end apart: 2 -> 0, of which waited for: 1 -> 0; matrix products, arithmetic and copies ran while one was open for 0% -> 0% of each run, Pallas kernels for 0% -> 0%
where the time goes in v2:
time: 89.8 us; the launch traced here: 89.5 us
  Pallas kernels  88.1 us (98%)
    pallas_call x1, Pallas kernels, shards(): pl.pallas_call(first_kernel, out_shape=(jax.ShapeDtypeStruct((devices, SL...  74.9 us
    pallas_call x1, Pallas kernels, shards(): pl.pallas_call(second_kernel, out_shape=(jax.ShapeDtypeStruct((rows_here,...  13.2 us

profile of v2, /device:TPU:1, one launch (start us, length us, event | category | flops | bytes accessed | tf_op | source)
XLA Modules:
  0.0 89.5 jit_solution(15048319184059834985)
XLA Ops:
  0.6 0.0 copy-start
  0.6 0.7 copy-done
  1.3 0.0 copy-start.1
  1.3 74.9 %first_block.1 = (bf16[128,8,512]{2,1,0:T(8,128)(2,1)S(1)}, s32[128,1,128]{2,1,0:T(1,128)S(1)}) custom-call(s32[3,8]{1,0:T(4,128)S(1)} %bitcast.5, bf16[8,64,512]{2,1,0:T(8,128)(2,1)} %bitcast.8, s32[1,512]{1,0:T(1,128)} %bitcast.9, f32[4,512]{1,0:T(4,128)} %gains_hbm.3, bf16[2,512,1536]{2,1,0:T(8,128)(2,1)} %qkv_hbm.3, bf16[2,512,512]{2,1,0:T(8,128)(2,1)} %proj_hbm.3, ...), custom_call_target="tpu_custom_call" | custom-call | flops 6442450944 | bytes 8388608 | tf_op jit(solution)/shard_map/first_block/pallas_call | solution.py:409
  76.3 0.0 copy-done.1
  76.3 13.2 %second_block.1 = (bf16[512,512]{1,0:T(8,128)(2,1)}, f32[3,512]{1,0:T(4,128)}) custom-call(s32[3,8]{1,0:T(4,128)S(1)} %bitcast.6, bf16[1024,512]{1,0:T(8,128)(2,1)S(1)} %bitcast.7, s32[128,1,128]{2,1,0:T(1,128)S(1)} %get-tuple-element.5.places, f32[4,512]{1,0:T(4,128)} %gains_hbm.3, bf16[3,512]{1,0:T(4,128)(2,1)} %head_hbm.1, bf16[2,512,1536]{2,1,0:T(8,128)(2,1)} %qkv_hbm.3, ...), custom_call_target="tpu_custom_call" | custom-call | flops 6442450944 | bytes 8388608 | tf_op jit(solution)/shard_map/second_block/pallas_call | solution.py:462
Async XLA Ops:
  0.6 0.7 copy-start
  1.3 75.0 %copy-start.1 = (s32[8,3]{0,1:T(4,128)S(1)}, s32[8,3]{0,1:T(4,128)}, u32[]{:S(2)}) copy-start(s32[8,3]{0,1:T(4,128)} %param.12) | copy-start | bytes 292

commit v3 on v2

--- a/solution.py
+++ b/solution.py
@@ -79,7 +79,7 @@
 def first_kernel(
     pattern, points_hbm, dest_hbm, gains_hbm, qkv_hbm, proj_hbm, up_hbm, down_hbm,
     incoming, in_places, points, dest, gains, asks, out_places, hx0, hx1, hx2, hx3, hz0, hz1, hz2, hz3, got_x, got_z, pats, send, table, picks,
-    chosen, q_ref, att_ref, acc_ref, outgoing, wq, wp, wu, wd, weight_sems,
+    chosen, q_ref, kv_ref, att_ref, acc_ref, outgoing, wq, wp, wu, wd, weight_sems,
     pat_sems, step_sems, send_sems, recv_sems, table_sem, ready_plane, ready_all, load_sems, row_sems, place_sems,
 ):
     grp = lax.axis_index("grp")
@@ -128,12 +128,26 @@
     held = ((hx0, hx1, hx2, hx3), (hz0, hz1, hz2, hz3))
     got = (got_x, got_z)
 
-    def first_step(axis, step):
+    def half_rows(part):
+        return pl.ds(part * (patches // 2), patches // 2)
+
+    def first_step(axis, step, part):
         return pltpu.make_async_remote_copy(
-            src_ref=points.at[:, :, pl.ds(axis * half, half)],
-            dst_ref=held[axis][SIDE - step],
-            send_sem=step_sems.at[axis, 0, step],
-            recv_sem=step_sems.at[axis, 1, SIDE - step],
+            src_ref=points.at[half_rows(part), :, pl.ds(axis * half, half)],
+            dst_ref=held[axis][SIDE - step].at[half_rows(part)],
+            send_sem=step_sems.at[axis, 0, step, part],
+            recv_sem=step_sems.at[axis, 1, SIDE - step, part],
+            device_id=at(axis, step, 0)[0],
+            device_id_type=MESH,
+        )
+
+    def relay(axis, part):
+        turn, step = ((SIDE - 1, 1), (1, SIDE - 1))[part]
+        return pltpu.make_async_remote_copy(
+            src_ref=held[axis][turn].at[half_rows(part)],
+            dst_ref=held[axis][2].at[half_rows(part)],
+            send_sem=step_sems.at[axis, 0, 2, part],
+            recv_sem=step_sems.at[axis, 1, 2, part],
             device_id=at(axis, step, 0)[0],
             device_id_type=MESH,
         )
@@ -151,9 +165,10 @@
     for peer in peers:
         ask(*peer, mine[peer[0]]).start()
     loads[0].wait()
-    for step in steps:
+    for early in (0, 1):
         for axis in (0, 1):
-            first_step(axis, step).start()
+            first_step(axis, 1, early).start()
+            first_step(axis, SIDE - 1, 1 - early).start()
     for step in steps:
         pl.semaphore_signal(ready_plane, inc=1, device_id=at(0, step, 0)[0], device_id_type=MESH)
     for axis in (0, 1):
@@ -178,6 +193,10 @@
     load = pltpu.make_async_copy(table, picks, table_sem)
     load.start()
     load.wait()
+    for axis in (0, 1):
+        for part in (0, 1):
+            first_step(axis, (1, SIDE - 1)[part], part).wait_recv()
+            relay(axis, part).start()
 
     def pass_on(axis, step, other, turn, k, place):
         return pltpu.make_async_remote_copy(
@@ -193,8 +212,11 @@
     for turn in (0,) + tuple(SIDE - step for step in steps):
         for axis in (0, 1):
             k = (along[axis] + turn) % SIDE
-            if turn:
-                first_step(axis, SIDE - turn).wait_recv()
+            if turn == 2:
+                for part in (0, 1):
+                    relay(axis, part).wait_recv()
+            elif turn:
+                first_step(axis, SIDE - turn, int(turn == SIDE - 1)).wait_recv()
             for step, other in askers:
                 row = (1 - axis) * places + at(1 - axis, step, other)[1]
                 for r in range(REQUESTS):
@@ -263,11 +285,15 @@
     gain = gains[0:1]
     rows = points[...].reshape(rows_here, channels)
     copies[0].wait()
-    q_ref[...] = mm(norm(rows, gain), wq[:, :channels]).astype(BF16)
+    hidden = norm(rows, gain)
+    q_ref[...] = mm(hidden, wq[:, :channels]).astype(BF16)
+    kv_ref[...] = mm(hidden, wq[:, channels:]).astype(BF16).reshape(patches, patch, 2 * channels)
 
     for axis in (0, 1):
-        for step in steps:
-            first_step(axis, step).wait_send()
+        for part in (0, 1):
+            first_step(axis, 1, part).wait_send()
+            first_step(axis, SIDE - 1, part).wait_send()
+            relay(axis, part).wait_send()
         for step, other in askers:
             if (step, other) != (0, 0):
                 for k in range(SIDE):
@@ -275,7 +301,6 @@
 
     owners = []
     for p in range(patches):
-        chosen[p, :patch] = points[p]
         for j in range(pattern.shape[0]):
             owner = named[p * pattern.shape[0] + j] >> 3
             r = jnp.int32(0)
@@ -284,20 +309,20 @@
             owners.append(owner)
             r = jnp.minimum(r, REQUESTS - 1)
             ox, oz, oc = owner // places, (owner // 2) % SIDE, owner % 2
-            to = slice((j + 1) * patch, (j + 2) * patch)
+            to = slice(j * patch, (j + 1) * patch)
             chosen[p, to, :half] = got_x[oz * 2 + oc, ox, r]
             chosen[p, to, half:] = got_z[ox * 2 + oc, oz, r]
 
     def one(p, carry):
         hidden = norm(chosen[p], gain)
-        kv = mm(hidden, wq[:, channels:]).astype(BF16)
+        kv = jnp.concatenate([kv_ref[p], mm(hidden, wq[:, channels:]).astype(BF16)], axis=0)
         start = pl.multiple_of(p * patch, patch)
         att_ref[pl.ds(start, patch)] = attend_patch(
             q_ref[pl.ds(start, patch)], kv[:, :channels], kv[:, channels:]
         )
         return carry
 
-    lax.fori_loop(0, patches, one, 0)
+    lax.fori_loop(0, patches, one, 0, unroll=True)
     done = finish(rows, att_ref, gains[1:2], wp, wu, wd, acc_ref, [copy.wait for copy in copies[1:]])
 
     for turn in range(SIDE):
@@ -370,7 +395,7 @@
         )
         return carry
 
-    lax.fori_loop(0, patches, one, 0)
+    lax.fori_loop(0, patches, one, 0, unroll=True)
     done = finish(
         rows_ref[...], att_ref, gains[3:4], wp, wu, wd, acc_ref, [copy.wait for copy in copies[1:]]
     )
@@ -428,8 +453,9 @@
             pltpu.VMEM((2, places, SIDE, REQUESTS, PATCH, half), BF16),
             pltpu.VMEM((2 * places, 128), jnp.int32),
             pltpu.SMEM((2 * places, 128), jnp.int32),
-            pltpu.VMEM((patches, 4 * PATCH, channels), BF16),
+            pltpu.VMEM((patches, pattern_first.shape[1] * PATCH, channels), BF16),
             pltpu.VMEM((rows_here, channels), BF16),
+            pltpu.VMEM((patches, PATCH, 2 * channels), BF16),
             pltpu.VMEM((rows_here, channels), BF16),
             pltpu.VMEM((rows_here, channels), F32),
             pltpu.VMEM((devices, SLOTS, channels), BF16),
@@ -437,7 +463,7 @@
         + weights
         + [
             pltpu.SemaphoreType.DMA((2, 2 * places)),
-            pltpu.SemaphoreType.DMA((2, 2, SIDE)),
+            pltpu.SemaphoreType.DMA((2, 2, SIDE, 2)),
             pltpu.SemaphoreType.DMA((2, places, SIDE)),
             pltpu.SemaphoreType.DMA((2, places, SIDE)),
             pltpu.SemaphoreType.DMA,

time: 89.8 us -> 80.2 us (0.89)
  Pallas kernels: 88.1 us -> 78.3 us
    pallas_call x1, Pallas kernels: 74.9 us -> 69.2 us  [shards(): pl.pallas_call(first_kernel, out_shape=(jax.ShapeDtypeStruct((devices, SL...]
    pallas_call x1, Pallas kernels: 13.2 us -> 9.04 us  [shards(): pl.pallas_call(second_kernel, out_shape=(jax.ShapeDtypeStruct((rows_here,...]
where the time goes in v3:
time: 80.2 us; the launch traced here: 79.8 us
  Pallas kernels  78.3 us (98%)
  between operations  0.82 us (1%)
    pallas_call x1, Pallas kernels, shards(): pl.pallas_call(first_kernel, out_shape=(jax.ShapeDtypeStruct((devices, SL...  69.2 us
    pallas_call x1, Pallas kernels, shards(): pl.pallas_call(second_kernel, out_shape=(jax.ShapeDtypeStruct((rows_here,...  9.04 us

profile of v3, /device:TPU:1, one launch (start us, length us, event | category | flops | bytes accessed | tf_op | source)
XLA Modules:
  0.0 79.8 jit_solution(16800855565772591089)
XLA Ops:
  0.6 0.0 copy-start
  0.6 0.7 copy-done
  1.3 0.0 copy-start.1
  1.3 69.2 %first_block.1 = (bf16[128,8,512]{2,1,0:T(8,128)(2,1)S(1)}, s32[128,1,128]{2,1,0:T(1,128)S(1)}) custom-call(s32[3,8]{1,0:T(4,128)S(1)} %bitcast.5, bf16[8,64,512]{2,1,0:T(8,128)(2,1)} %bitcast.8, s32[1,512]{1,0:T(1,128)} %bitcast.9, f32[4,512]{1,0:T(4,128)} %gains_hbm.3, bf16[2,512,1536]{2,1,0:T(8,128)(2,1)} %qkv_hbm.3, bf16[2,512,512]{2,1,0:T(8,128)(2,1)} %proj_hbm.3, ...), custom_call_target="tpu_custom_call" | custom-call | flops 6442450944 | bytes 8388608 | tf_op jit(solution)/shard_map/first_block/pallas_call | solution.py:434
  70.6 0.0 copy-done.1
  70.6 9.0 %second_block.1 = (bf16[512,512]{1,0:T(8,128)(2,1)}, f32[3,512]{1,0:T(4,128)}) custom-call(s32[3,8]{1,0:T(4,128)S(1)} %bitcast.6, bf16[1024,512]{1,0:T(8,128)(2,1)S(1)} %bitcast.7, s32[128,1,128]{2,1,0:T(1,128)S(1)} %get-tuple-element.5.places, f32[4,512]{1,0:T(4,128)} %gains_hbm.3, bf16[3,512]{1,0:T(4,128)(2,1)} %head_hbm.1, bf16[2,512,1536]{2,1,0:T(8,128)(2,1)} %qkv_hbm.3, ...), custom_call_target="tpu_custom_call" | custom-call | flops 6442450944 | bytes 8388608 | tf_op jit(solution)/shard_map/second_block/pallas_call | solution.py:488
Async XLA Ops:
  0.6 0.7 copy-start
  1.3 69.2 %copy-start.1 = (s32[8,3]{0,1:T(4,128)S(1)}, s32[8,3]{0,1:T(4,128)}, u32[]{:S(2)}) copy-start(s32[8,3]{0,1:T(4,128)} %param.12) | copy-start | bytes 292

commit v4 on v3

--- a/solution.py
+++ b/solution.py
@@ -76,9 +76,28 @@
     ]
 
 
+def places_by_slot(places):
+    devices = places.shape[0]
+    slots = devices * SLOTS
+    table = jnp.transpose(places)[:SLOTS]
+    spread = (
+        lax.broadcasted_iota(jnp.int32, (devices, slots), 1) // SLOTS
+        == lax.broadcasted_iota(jnp.int32, (devices, slots), 0)
+    ).astype(BF16)
+    high = mm((table >> 4).astype(F32).astype(BF16), spread)
+    low = mm((table & 15).astype(F32).astype(BF16), spread)
+    of_rank = (
+        lax.broadcasted_iota(jnp.int32, (SLOTS, slots), 1) % SLOTS
+        == lax.broadcasted_iota(jnp.int32, (SLOTS, slots), 0)
+    )
+    return jnp.sum(
+        jnp.where(of_rank, high * 16.0 + low, 0.0), axis=0, keepdims=True
+    ).astype(jnp.int32)
+
+
 def first_kernel(
-    pattern, points_hbm, dest_hbm, gains_hbm, qkv_hbm, proj_hbm, up_hbm, down_hbm,
-    incoming, in_places, points, dest, gains, asks, out_places, hx0, hx1, hx2, hx3, hz0, hz1, hz2, hz3, got_x, got_z, pats, send, table, picks,
+    pattern_hbm, points_hbm, dest_hbm, gains_hbm, qkv_hbm, proj_hbm, up_hbm, down_hbm,
+    incoming, recv_match, pattern, points, dest, gains, asks, out_places, in_places, send_match, hx0, hx1, hx2, hx3, hz0, hz1, hz2, hz3, got_x, got_z, pats, send, table, picks,
     chosen, q_ref, kv_ref, att_ref, acc_ref, outgoing, wq, wp, wu, wd, weight_sems,
     pat_sems, step_sems, send_sems, recv_sems, table_sem, ready_plane, ready_all, load_sems, row_sems, place_sems,
 ):
@@ -90,17 +109,13 @@
     places = 2 * SIDE
     loads = [
         pltpu.make_async_copy(source, target, load_sems.at[n])
-        for n, (source, target) in enumerate(((points_hbm, points), (dest_hbm, dest), (gains_hbm, gains)))
+        for n, (source, target) in enumerate(
+            ((pattern_hbm, pattern), (points_hbm, points), (dest_hbm, dest), (gains_hbm, gains))
+        )
     ]
     copies = weight_copies(0, (qkv_hbm, proj_hbm, up_hbm, down_hbm), (wq, wp, wu, wd), weight_sems)
     for copy in loads + copies:
         copy.start()
-    lane = lax.broadcasted_iota(jnp.int32, asks.shape, 1)
-    asking = jnp.full(asks.shape, -1, jnp.int32)
-    named = [pattern[j, p] for p in range(patches) for j in range(pattern.shape[0])]
-    for n, name in enumerate(named):
-        asking = jnp.where(lane == n, name, asking)
-    asks[...] = asking
 
     def at(axis, step, other):
         core = (c + other) % 2
@@ -121,6 +136,13 @@
         pl.semaphore_signal(barrier, inc=1, device_id=at(*peer)[0], device_id_type=MESH)
     for step in steps:
         pl.semaphore_signal(barrier, inc=1, device_id=across(step), device_id_type=MESH)
+    loads[0].wait()
+    lane = lax.broadcasted_iota(jnp.int32, asks.shape, 1)
+    asking = jnp.full(asks.shape, -1, jnp.int32)
+    named = [pattern[j, p] for p in range(patches) for j in range(pattern.shape[0])]
+    for n, name in enumerate(named):
+        asking = jnp.where(lane == n, name, asking)
+    asks[...] = asking
     pl.semaphore_wait(barrier, len(peers) + len(steps))
 
     along = (x, z)
@@ -164,7 +186,7 @@
 
     for peer in peers:
         ask(*peer, mine[peer[0]]).start()
-    loads[0].wait()
+    loads[1].wait()
     for early in (0, 1):
         for axis in (0, 1):
             first_step(axis, 1, early).start()
@@ -233,8 +255,8 @@
 
     rows_here = patches * patch
     devices = incoming.shape[0]
-    loads[1].wait()
     loads[2].wait()
+    loads[3].wait()
     target = dest[...] >> 9
     on_device = lax.broadcasted_iota(jnp.int32, (devices, rows_here), 0) == target
     before = lax.broadcasted_iota(jnp.int32, (rows_here, rows_here), 0) < lax.broadcasted_iota(
@@ -288,6 +310,20 @@
     hidden = norm(rows, gain)
     q_ref[...] = mm(hidden, wq[:, :channels]).astype(BF16)
     kv_ref[...] = mm(hidden, wq[:, channels:]).astype(BF16).reshape(patches, patch, 2 * channels)
+
+    def device_at(dy, n):
+        dx, dz, dc = n // (2 * SIDE), (n // 2) % SIDE, n % 2
+        number = ((x + dx) % SIDE * SIDE + (z + dz) % SIDE) * 2 + (c + dc) % 2
+        return (grp + dy) % SIDE, number
+
+    def far(dy, n):
+        return sum(min(d, SIDE - d) for d in (dy, n // (2 * SIDE), (n // 2) % SIDE))
+
+    for dy in range(SIDE):
+        row = lax.broadcasted_iota(jnp.int32, (group * SLOTS, 1), 0)
+        to_grp, number = device_at(dy, row // SLOTS)
+        wanted = (to_grp * group + number) * SLOTS + row % SLOTS
+        send_match[dy * group * SLOTS : (dy + 1) * group * SLOTS] = (wanted == slot).astype(BF16)
 
     for axis in (0, 1):
         for part in (0, 1):
@@ -325,33 +361,41 @@
     lax.fori_loop(0, patches, one, 0, unroll=True)
     done = finish(rows, att_ref, gains[1:2], wp, wu, wd, acc_ref, [copy.wait for copy in copies[1:]])
 
-    for turn in range(SIDE):
-        to_grp = (grp + turn) % SIDE
-        match = (
-            lax.broadcasted_iota(jnp.int32, (group * SLOTS, rows_here), 0) + to_grp * (group * SLOTS) == slot
-        )
-        outgoing[pl.ds(to_grp * group, group)] = (
-            mm(match.astype(BF16), done).astype(BF16).reshape(group, SLOTS, channels)
-        )
-
-        def send_rows(k, carry):
-            send_to(outgoing, incoming, row_sems, to_grp * group + (seq + k) % group).start()
-            return carry
-
-        lax.fori_loop(1 if turn == 0 else 0, group, send_rows, 0)
-    incoming[me] = outgoing[me]
+    for dy in range(SIDE):
+        outgoing[dy * group : (dy + 1) * group] = (
+            mm(send_match[dy * group * SLOTS : (dy + 1) * group * SLOTS], done)
+            .astype(BF16)
+            .reshape(group, SLOTS, channels)
+        )
+    for dy, n in sorted([(dy, n) for dy in range(SIDE) for n in range(group)], key=lambda to: -far(*to)):
+        if (dy, n) != (0, 0):
+            pltpu.make_async_remote_copy(
+                src_ref=outgoing.at[dy * group + n],
+                dst_ref=incoming.at[me],
+                send_sem=row_sems.at[0],
+                recv_sem=row_sems.at[1],
+                device_id=device_at(dy, n),
+                device_id_type=MESH,
+            ).start()
+    incoming[me] = outgoing[0]
+
     arrive(out_places, in_places, place_sems)
+    slot_place = places_by_slot(in_places[...].reshape(devices, 128))
+    step = 128
+    for start in range(0, rows_here, step):
+        place_of = lax.broadcasted_iota(jnp.int32, (step, devices * SLOTS), 0) + (start + 1)
+        recv_match[start : start + step] = (place_of == slot_place).astype(BF16)
     arrive(outgoing, incoming, row_sems)
 
 
 def second_kernel(
-    pattern, incoming, places, gains_hbm, head_hbm, qkv_hbm, proj_hbm, up_hbm, down_hbm,
-    features, normals, gains, head, rows_ref, q_ref, kv_ref, att_ref, acc_ref, wq, wp, wu, wd, sems, load_sems,
+    pattern_hbm, incoming, match, gains_hbm, head_hbm, qkv_hbm, proj_hbm, up_hbm, down_hbm,
+    features, normals, pattern, gains, head, rows_ref, q_ref, kv_ref, att_ref, acc_ref, wq, wp, wu, wd, sems, load_sems,
 ):
     loads = [
         pltpu.make_async_copy(source, target, load_sems.at[n])
         for n, (source, target) in enumerate(
-            ((gains_hbm, gains), (head_hbm, head))
+            ((gains_hbm, gains), (head_hbm, head), (pattern_hbm, pattern))
         )
     ]
     copies = weight_copies(1, (qkv_hbm, proj_hbm, up_hbm, down_hbm), (wq, wp, wu, wd), sems)
@@ -359,26 +403,7 @@
         copy.start()
     picks, patches = pattern.shape
     rows_here, channels = features.shape
-    devices = places.shape[0]
-    slots = devices * SLOTS
-    table = jnp.transpose(places[...].reshape(devices, 128))[:SLOTS]
-    spread = (
-        lax.broadcasted_iota(jnp.int32, (devices, slots), 1) // SLOTS
-        == lax.broadcasted_iota(jnp.int32, (devices, slots), 0)
-    ).astype(BF16)
-    high = mm((table >> 4).astype(F32).astype(BF16), spread)
-    low = mm((table & 15).astype(F32).astype(BF16), spread)
-    of_rank = (
-        lax.broadcasted_iota(jnp.int32, (SLOTS, slots), 1) % SLOTS
-        == lax.broadcasted_iota(jnp.int32, (SLOTS, slots), 0)
-    )
-    slot_place = jnp.sum(
-        jnp.where(of_rank, high * 16.0 + low, 0.0), axis=0, keepdims=True
-    ).astype(jnp.int32)
-    step = 256
-    for at in range(0, rows_here, step):
-        match = lax.broadcasted_iota(jnp.int32, (step, slots), 0) + (at + 1) == slot_place
-        rows_ref[at : at + step] = mm(match.astype(BF16), incoming[...]).astype(BF16)
+    rows_ref[...] = mm(match[...], incoming[...]).astype(BF16)
     loads[0].wait()
     copies[0].wait()
     hidden = norm(rows_ref[...], gains[2:3])
@@ -386,6 +411,8 @@
     kv_ref[...] = (
         mm(hidden, wq[:, channels:]).astype(BF16).reshape(patches, PATCH, 2 * channels)
     )
+
+    loads[2].wait()
 
     def one(p, carry):
         kv = jnp.concatenate([kv_ref[p]] + [kv_ref[pattern[j, p]] for j in range(picks)], axis=0)
@@ -415,7 +442,6 @@
     devices = lax.axis_size("grp") * lax.axis_size("seq")
     slots = devices * SLOTS
     vmem = pl.BlockSpec(memory_space=pltpu.VMEM)
-    smem = pl.BlockSpec(memory_space=pltpu.SMEM)
     hbm = pl.BlockSpec(memory_space=pltpu.HBM)
     weights = [
         pltpu.VMEM((channels, 3 * channels), BF16),
@@ -431,20 +457,23 @@
     half = channels // 2
     keep = lambda array: pltpu.with_memory_space_constraint(array, pltpu.HBM)
     stacks = [keep(array) for array in (w_qkv, w_proj, w_up, w_down)]
-    incoming, places_in = pl.pallas_call(
+    incoming, match = pl.pallas_call(
         first_kernel,
         out_shape=(
             jax.ShapeDtypeStruct((devices, SLOTS, channels), BF16),
-            jax.ShapeDtypeStruct((devices, 1, 128), jnp.int32),
+            jax.ShapeDtypeStruct((rows_here, slots), BF16),
         ),
-        in_specs=[smem] + [hbm] * 7,
+        in_specs=[hbm] * 8,
         out_specs=(vmem, vmem),
         scratch_shapes=[
+            pltpu.SMEM(pattern_first.shape[::-1], jnp.int32),
             pltpu.VMEM((patches, PATCH, channels), BF16),
             pltpu.VMEM((1, rows_here), jnp.int32),
             pltpu.VMEM(norm_gains.shape, F32),
             pltpu.VMEM((1, 128), jnp.int32),
             pltpu.VMEM((devices, 1, 128), jnp.int32),
+            pltpu.VMEM((devices, 1, 128), jnp.int32),
+            pltpu.VMEM((slots, rows_here), BF16),
         ]
         + [pltpu.VMEM((patches, PATCH, half), BF16)] * (2 * SIDE)
         + [pltpu.VMEM((places, SIDE, REQUESTS, PATCH, half), BF16)] * 2
@@ -469,7 +498,7 @@
             pltpu.SemaphoreType.DMA,
             pltpu.SemaphoreType.REGULAR,
             pltpu.SemaphoreType.REGULAR,
-            pltpu.SemaphoreType.DMA((3,)),
+            pltpu.SemaphoreType.DMA((4,)),
             pltpu.SemaphoreType.DMA((2,)),
             pltpu.SemaphoreType.DMA((2,)),
         ],
@@ -479,7 +508,7 @@
         cost_estimate=cost,
         name="first_block",
     )(
-        pattern_first.T,
+        keep(pattern_first.T),
         keep(points.reshape(patches, PATCH, channels)),
         keep(destination.reshape(1, rows_here)),
         keep(norm_gains),
@@ -491,9 +520,10 @@
             jax.ShapeDtypeStruct((rows_here, channels), BF16),
             jax.ShapeDtypeStruct((w_head.shape[0], rows_here), F32),
         ),
-        in_specs=[smem, vmem, vmem] + [hbm] * 6,
+        in_specs=[hbm, vmem, vmem] + [hbm] * 6,
         out_specs=(vmem, vmem),
         scratch_shapes=[
+            pltpu.SMEM(pattern_second.shape[::-1], jnp.int32),
             pltpu.VMEM(norm_gains.shape, F32),
             pltpu.VMEM(w_head.shape, BF16),
             pltpu.VMEM((rows_here, channels), BF16),
@@ -503,14 +533,14 @@
             pltpu.VMEM((rows_here, channels), F32),
         ]
         + weights
-        + [pltpu.SemaphoreType.DMA((2,))],
+        + [pltpu.SemaphoreType.DMA((3,))],
         compiler_params=params,
         cost_estimate=cost,
         name="second_block",
     )(
-        pattern_second.T,
+        keep(pattern_second.T),
         incoming.reshape(slots, channels),
-        places_in,
+        match,
         keep(norm_gains),
         keep(w_head),
         *stacks,

time: 80.2 us -> 77.3 us (0.964)
  Pallas kernels: 78.3 us -> 76.3 us
    pallas_call x1, Pallas kernels: 69.2 us -> 67.2 us  [shards(): pl.pallas_call(first_kernel, out_shape=(jax.ShapeDtypeStruct((devices, SL...]
where the time goes in v4:
time: 77.3 us; the launch traced here: 77.1 us
  Pallas kernels  76.3 us (99%)
  between operations  0.8 us (1%)
    pallas_call x1, Pallas kernels, shards(): pl.pallas_call(first_kernel, out_shape=(jax.ShapeDtypeStruct((devices, SL...  67.2 us
    pallas_call x1, Pallas kernels, shards(): pl.pallas_call(second_kernel, out_shape=(jax.ShapeDtypeStruct((rows_here,...  9.17 us

profile of v4, /device:TPU:1, one launch (start us, length us, event | category | flops | bytes accessed | tf_op | source)
XLA Modules:
  0.0 77.1 jit_solution(11247906031897291100)
XLA Ops:
  0.6 67.2 %first_block.1 = (bf16[128,8,512]{2,1,0:T(8,128)(2,1)S(1)}, bf16[512,1024]{1,0:T(8,128)(2,1)S(1)}) custom-call(s32[3,8]{1,0:T(4,128)} %bitcast.7, bf16[8,64,512]{2,1,0:T(8,128)(2,1)} %bitcast.6, s32[1,512]{1,0:T(1,128)} %bitcast.8, f32[4,512]{1,0:T(4,128)} %gains_hbm.3, bf16[2,512,1536]{2,1,0:T(8,128)(2,1)} %qkv_hbm.3, bf16[2,512,512]{2,1,0:T(8,128)(2,1)} %proj_hbm.3, ...), custom_call_target="tpu_custom_call" | custom-call | flops 6442450944 | bytes 8388608 | tf_op jit(solution)/shard_map/first_block/pallas_call | solution.py:460
  67.8 9.2 %second_block.1 = (bf16[512,512]{1,0:T(8,128)(2,1)}, f32[3,512]{1,0:T(4,128)}) custom-call(s32[3,8]{1,0:T(4,128)} %bitcast.9, bf16[1024,512]{1,0:T(8,128)(2,1)S(1)} %bitcast.5, bf16[512,1024]{1,0:T(8,128)(2,1)S(1)} %get-tuple-element.5.match, f32[4,512]{1,0:T(4,128)} %gains_hbm.3, bf16[3,512]{1,0:T(4,128)(2,1)} %head_hbm.1, bf16[2,512,1536]{2,1,0:T(8,128)(2,1)} %qkv_hbm.3, ...), custom_call_target="tpu_custom_call" | custom-call | flops 6442450944 | bytes 8388608 | tf_op jit(solution)/shard_map/second_block/pallas_call | solution.py:517

commit v5 on v4

--- a/solution.py
+++ b/solution.py
@@ -53,13 +53,14 @@
     return jnp.concatenate(mixed, axis=1).astype(BF16)
 
 
-def finish(rows, att_ref, gains, wp_ref, wu_ref, wd_ref, acc_ref, waits):
-    waits[0]()
+def finish(rows, att_ref, gains, wp_ref, wu_ref, wd_ref, acc_ref, waits=()):
+    for wait in waits[:1]:
+        wait()
     first = (rows.astype(F32) + mm(att_ref[...], wp_ref[...])).astype(BF16)
     hidden = norm(first, gains)
     acc_ref[...] = first.astype(F32)
-    waits[1]()
-    waits[2]()
+    for wait in waits[1:]:
+        wait()
     ff = wu_ref.shape[1]
     step = 512
     for at in range(0, ff, step):
@@ -97,8 +98,8 @@
 
 def first_kernel(
     pattern_hbm, points_hbm, dest_hbm, gains_hbm, qkv_hbm, proj_hbm, up_hbm, down_hbm,
-    incoming, recv_match, pattern, points, dest, gains, asks, out_places, in_places, send_match, hx0, hx1, hx2, hx3, hz0, hz1, hz2, hz3, got_x, got_z, pats, send, table, picks,
-    chosen, q_ref, kv_ref, att_ref, acc_ref, outgoing, wq, wp, wu, wd, weight_sems,
+    incoming, recv_match, next_wq, next_wp, next_wu, next_wd, pattern, points, dest, gains, asks, out_places, in_places, send_match, hx0, hx1, hx2, hx3, hz0, hz1, hz2, hz3, got_x, got_z, pats, send, table, picks,
+    normed, q_ref, kv_ref, att_ref, acc_ref, outgoing, wq, wp, wu, wd, weight_sems, next_sems,
     pat_sems, step_sems, send_sems, recv_sems, table_sem, ready_plane, ready_all, load_sems, row_sems, place_sems,
 ):
     grp = lax.axis_index("grp")
@@ -107,15 +108,18 @@
     patches, patch, channels = points.shape
     half = channels // 2
     places = 2 * SIDE
+    rows_here = patches * patch
     loads = [
         pltpu.make_async_copy(source, target, load_sems.at[n])
         for n, (source, target) in enumerate(
             ((pattern_hbm, pattern), (points_hbm, points), (dest_hbm, dest), (gains_hbm, gains))
         )
     ]
-    copies = weight_copies(0, (qkv_hbm, proj_hbm, up_hbm, down_hbm), (wq, wp, wu, wd), weight_sems)
-    for copy in loads + copies:
-        copy.start()
+    for load in loads:
+        load.start()
+    stacks = (qkv_hbm, proj_hbm, up_hbm, down_hbm)
+    copies = weight_copies(0, stacks, (wq, wp, wu, wd), weight_sems)
+    next_copies = weight_copies(1, stacks, (next_wq, next_wp, next_wu, next_wd), next_sems)
 
     def at(axis, step, other):
         core = (c + other) % 2
@@ -136,7 +140,10 @@
         pl.semaphore_signal(barrier, inc=1, device_id=at(*peer)[0], device_id_type=MESH)
     for step in steps:
         pl.semaphore_signal(barrier, inc=1, device_id=across(step), device_id_type=MESH)
-    loads[0].wait()
+    for load in loads:
+        load.wait()
+    rows = points[...].reshape(rows_here, channels)
+    normed[...] = norm(rows, gains[0:1]).reshape(patches, patch, channels)
     lane = lax.broadcasted_iota(jnp.int32, asks.shape, 1)
     asking = jnp.full(asks.shape, -1, jnp.int32)
     named = [pattern[j, p] for p in range(patches) for j in range(pattern.shape[0])]
@@ -155,7 +162,7 @@
 
     def first_step(axis, step, part):
         return pltpu.make_async_remote_copy(
-            src_ref=points.at[half_rows(part), :, pl.ds(axis * half, half)],
+            src_ref=normed.at[half_rows(part), :, pl.ds(axis * half, half)],
             dst_ref=held[axis][SIDE - step].at[half_rows(part)],
             send_sem=step_sems.at[axis, 0, step, part],
             recv_sem=step_sems.at[axis, 1, SIDE - step, part],
@@ -186,15 +193,16 @@
 
     for peer in peers:
         ask(*peer, mine[peer[0]]).start()
-    loads[1].wait()
     for early in (0, 1):
         for axis in (0, 1):
             first_step(axis, 1, early).start()
             first_step(axis, SIDE - 1, 1 - early).start()
+    for copy in copies:
+        copy.start()
     for step in steps:
         pl.semaphore_signal(ready_plane, inc=1, device_id=at(0, step, 0)[0], device_id_type=MESH)
     for axis in (0, 1):
-        held[axis][0][...] = points[:, :, axis * half : (axis + 1) * half]
+        held[axis][0][...] = normed[:, :, axis * half : (axis + 1) * half]
         pats[axis * places + mine[axis]] = asks[...]
     for peer in peers:
         ask(*peer, at(*peer)[1]).wait()
@@ -230,7 +238,7 @@
             device_id_type=MESH,
         )
 
-    askers = [(step, other) for step in steps + (0,) for other in (0, 1)]
+    askers = [(step, other) for step in (2, 1, SIDE - 1, 0) for other in (1, 0)]
     for turn in (0,) + tuple(SIDE - step for step in steps):
         for axis in (0, 1):
             k = (along[axis] + turn) % SIDE
@@ -253,10 +261,7 @@
     for step in steps:
         pl.semaphore_signal(ready_all, inc=1, device_id=across(step), device_id_type=MESH)
 
-    rows_here = patches * patch
     devices = incoming.shape[0]
-    loads[2].wait()
-    loads[3].wait()
     target = dest[...] >> 9
     on_device = lax.broadcasted_iota(jnp.int32, (devices, rows_here), 0) == target
     before = lax.broadcasted_iota(jnp.int32, (rows_here, rows_here), 0) < lax.broadcasted_iota(
@@ -304,26 +309,30 @@
 
     lax.fori_loop(1, devices, send_places, 0)
     in_places[me] = out_places[me]
-    gain = gains[0:1]
-    rows = points[...].reshape(rows_here, channels)
     copies[0].wait()
-    hidden = norm(rows, gain)
+    hidden = normed[...].reshape(rows_here, channels)
     q_ref[...] = mm(hidden, wq[:, :channels]).astype(BF16)
     kv_ref[...] = mm(hidden, wq[:, channels:]).astype(BF16).reshape(patches, patch, 2 * channels)
-
-    def device_at(dy, n):
-        dx, dz, dc = n // (2 * SIDE), (n // 2) % SIDE, n % 2
+    for copy in next_copies:
+        copy.start()
+
+    def device_at(step):
+        dy, dx, dz, dc = step
         number = ((x + dx) % SIDE * SIDE + (z + dz) % SIDE) * 2 + (c + dc) % 2
         return (grp + dy) % SIDE, number
 
-    def far(dy, n):
-        return sum(min(d, SIDE - d) for d in (dy, n // (2 * SIDE), (n // 2) % SIDE))
-
-    for dy in range(SIDE):
-        row = lax.broadcasted_iota(jnp.int32, (group * SLOTS, 1), 0)
-        to_grp, number = device_at(dy, row // SLOTS)
-        wanted = (to_grp * group + number) * SLOTS + row % SLOTS
-        send_match[dy * group * SLOTS : (dy + 1) * group * SLOTS] = (wanted == slot).astype(BF16)
+    def near(step):
+        return -sum(min(d, SIDE - d) for d in step[:3]), step
+
+    ways = range(SIDE)
+    order = sorted([(dy, dx, dz, dc) for dy in ways for dx in ways for dz in ways for dc in (0, 1)], key=near)
+    order.remove((0, 0, 0, 0))
+    order.append((0, 0, 0, 0))
+    row = lax.broadcasted_iota(jnp.int32, (2 * SLOTS, rows_here), 0)
+    for n in range(0, devices, 2):
+        one, two = ((to_grp * group + number) * SLOTS for to_grp, number in map(device_at, order[n : n + 2]))
+        wanted = jnp.where(row < SLOTS, one + row, two - SLOTS + row)
+        send_match[n * SLOTS : (n + 2) * SLOTS] = (wanted == slot).astype(BF16)
 
     for axis in (0, 1):
         for part in (0, 1):
@@ -335,49 +344,46 @@
                 for k in range(SIDE):
                     pass_on(axis, step, other, k, k, at(1 - axis, step, other)[1]).wait()
 
+    picks_here = pattern.shape[0]
     owners = []
     for p in range(patches):
-        for j in range(pattern.shape[0]):
-            owner = named[p * pattern.shape[0] + j] >> 3
+        parts = []
+        for j in range(picks_here):
+            owner = named[p * picks_here + j] >> 3
             r = jnp.int32(0)
             for earlier_owner in owners:
                 r = r + jnp.where(earlier_owner == owner, 1, 0)
             owners.append(owner)
             r = jnp.minimum(r, REQUESTS - 1)
             ox, oz, oc = owner // places, (owner // 2) % SIDE, owner % 2
-            to = slice(j * patch, (j + 1) * patch)
-            chosen[p, to, :half] = got_x[oz * 2 + oc, ox, r]
-            chosen[p, to, half:] = got_z[ox * 2 + oc, oz, r]
-
-    def one(p, carry):
-        hidden = norm(chosen[p], gain)
-        kv = jnp.concatenate([kv_ref[p], mm(hidden, wq[:, channels:]).astype(BF16)], axis=0)
-        start = pl.multiple_of(p * patch, patch)
-        att_ref[pl.ds(start, patch)] = attend_patch(
-            q_ref[pl.ds(start, patch)], kv[:, :channels], kv[:, channels:]
-        )
-        return carry
-
-    lax.fori_loop(0, patches, one, 0, unroll=True)
+            parts.append(
+                jnp.concatenate([got_x[oz * 2 + oc, ox, r], got_z[ox * 2 + oc, oz, r]], axis=1)
+            )
+        chosen = jnp.concatenate(parts, axis=0)
+        kv = jnp.concatenate([kv_ref[p], mm(chosen, wq[:, channels:]).astype(BF16)], axis=0)
+        att_ref[p * patch : (p + 1) * patch] = attend_patch(
+            q_ref[p * patch : (p + 1) * patch], kv[:, :channels], kv[:, channels:]
+        )
+
     done = finish(rows, att_ref, gains[1:2], wp, wu, wd, acc_ref, [copy.wait for copy in copies[1:]])
 
-    for dy in range(SIDE):
-        outgoing[dy * group : (dy + 1) * group] = (
-            mm(send_match[dy * group * SLOTS : (dy + 1) * group * SLOTS], done)
+    for quarter in range(SIDE):
+        start = quarter * group
+        outgoing[start : start + group] = (
+            mm(send_match[start * SLOTS : (start + group) * SLOTS], done)
             .astype(BF16)
             .reshape(group, SLOTS, channels)
         )
-    for dy, n in sorted([(dy, n) for dy in range(SIDE) for n in range(group)], key=lambda to: -far(*to)):
-        if (dy, n) != (0, 0):
+        for n in range(start, min(start + group, devices - 1)):
             pltpu.make_async_remote_copy(
-                src_ref=outgoing.at[dy * group + n],
+                src_ref=outgoing.at[n],
                 dst_ref=incoming.at[me],
                 send_sem=row_sems.at[0],
                 recv_sem=row_sems.at[1],
-                device_id=device_at(dy, n),
+                device_id=device_at(order[n]),
                 device_id_type=MESH,
             ).start()
-    incoming[me] = outgoing[0]
+    incoming[me] = outgoing[devices - 1]
 
     arrive(out_places, in_places, place_sems)
     slot_place = places_by_slot(in_places[...].reshape(devices, 128))
@@ -385,12 +391,14 @@
     for start in range(0, rows_here, step):
         place_of = lax.broadcasted_iota(jnp.int32, (step, devices * SLOTS), 0) + (start + 1)
         recv_match[start : start + step] = (place_of == slot_place).astype(BF16)
+    for copy in next_copies:
+        copy.wait()
     arrive(outgoing, incoming, row_sems)
 
 
 def second_kernel(
-    pattern_hbm, incoming, match, gains_hbm, head_hbm, qkv_hbm, proj_hbm, up_hbm, down_hbm,
-    features, normals, pattern, gains, head, rows_ref, q_ref, kv_ref, att_ref, acc_ref, wq, wp, wu, wd, sems, load_sems,
+    pattern_hbm, incoming, match, gains_hbm, head_hbm, wq, wp, wu, wd,
+    features, normals, pattern, gains, head, rows_ref, q_ref, kv_ref, att_ref, acc_ref, load_sems,
 ):
     loads = [
         pltpu.make_async_copy(source, target, load_sems.at[n])
@@ -398,14 +406,12 @@
             ((gains_hbm, gains), (head_hbm, head), (pattern_hbm, pattern))
         )
     ]
-    copies = weight_copies(1, (qkv_hbm, proj_hbm, up_hbm, down_hbm), (wq, wp, wu, wd), sems)
-    for copy in loads + copies:
-        copy.start()
+    for load in loads:
+        load.start()
     picks, patches = pattern.shape
     rows_here, channels = features.shape
     rows_ref[...] = mm(match[...], incoming[...]).astype(BF16)
     loads[0].wait()
-    copies[0].wait()
     hidden = norm(rows_ref[...], gains[2:3])
     q_ref[...] = mm(hidden, wq[:, :channels]).astype(BF16)
     kv_ref[...] = (
@@ -424,7 +430,7 @@
 
     lax.fori_loop(0, patches, one, 0, unroll=True)
     done = finish(
-        rows_ref[...], att_ref, gains[3:4], wp, wu, wd, acc_ref, [copy.wait for copy in copies[1:]]
+        rows_ref[...], att_ref, gains[3:4], wp, wu, wd, acc_ref
     )
     features[...] = done
     loads[1].wait()
@@ -448,23 +454,23 @@
         pltpu.VMEM((channels, channels), BF16),
         pltpu.VMEM((channels, ff), BF16),
         pltpu.VMEM((ff, channels), BF16),
-        pltpu.SemaphoreType.DMA((4,)),
     ]
-    params = pltpu.CompilerParams(vmem_limit_bytes=48 << 20)
+    params = pltpu.CompilerParams(vmem_limit_bytes=24 << 20)
     work = 2 * rows_here * channels * (4 * channels + 2 * ff)
     cost = pl.CostEstimate(flops=2 * work, bytes_accessed=8 << 20, transcendentals=rows_here * ff)
     places = 2 * SIDE
     half = channels // 2
     keep = lambda array: pltpu.with_memory_space_constraint(array, pltpu.HBM)
     stacks = [keep(array) for array in (w_qkv, w_proj, w_up, w_down)]
-    incoming, match = pl.pallas_call(
+    incoming, match, *next_weights = pl.pallas_call(
         first_kernel,
         out_shape=(
             jax.ShapeDtypeStruct((devices, SLOTS, channels), BF16),
             jax.ShapeDtypeStruct((rows_here, slots), BF16),
+            *(jax.ShapeDtypeStruct(stack.shape[1:], BF16) for stack in stacks),
         ),
         in_specs=[hbm] * 8,
-        out_specs=(vmem, vmem),
+        out_specs=(vmem,) * 6,
         scratch_shapes=[
             pltpu.SMEM(pattern_first.shape[::-1], jnp.int32),
             pltpu.VMEM((patches, PATCH, channels), BF16),
@@ -482,7 +488,7 @@
             pltpu.VMEM((2, places, SIDE, REQUESTS, PATCH, half), BF16),
             pltpu.VMEM((2 * places, 128), jnp.int32),
             pltpu.SMEM((2 * places, 128), jnp.int32),
-            pltpu.VMEM((patches, pattern_first.shape[1] * PATCH, channels), BF16),
+            pltpu.VMEM((patches, PATCH, channels), BF16),
             pltpu.VMEM((rows_here, channels), BF16),
             pltpu.VMEM((patches, PATCH, 2 * channels), BF16),
             pltpu.VMEM((rows_here, channels), BF16),
@@ -491,6 +497,8 @@
         ]
         + weights
         + [
+            pltpu.SemaphoreType.DMA((4,)),
+            pltpu.SemaphoreType.DMA((4,)),
             pltpu.SemaphoreType.DMA((2, 2 * places)),
             pltpu.SemaphoreType.DMA((2, 2, SIDE, 2)),
             pltpu.SemaphoreType.DMA((2, places, SIDE)),
@@ -503,7 +511,7 @@
             pltpu.SemaphoreType.DMA((2,)),
         ],
         compiler_params=pltpu.CompilerParams(
-            vmem_limit_bytes=48 << 20, collective_id=0, has_side_effects=True
+            vmem_limit_bytes=32 << 20, collective_id=0, has_side_effects=True
         ),
         cost_estimate=cost,
         name="first_block",
@@ -520,7 +528,7 @@
             jax.ShapeDtypeStruct((rows_here, channels), BF16),
             jax.ShapeDtypeStruct((w_head.shape[0], rows_here), F32),
         ),
-        in_specs=[hbm, vmem, vmem] + [hbm] * 6,
+        in_specs=[hbm, vmem, vmem, hbm, hbm] + [vmem] * 4,
         out_specs=(vmem, vmem),
         scratch_shapes=[
             pltpu.SMEM(pattern_second.shape[::-1], jnp.int32),
@@ -532,7 +540,6 @@
             pltpu.VMEM((rows_here, channels), BF16),
             pltpu.VMEM((rows_here, channels), F32),
         ]
-        + weights
         + [pltpu.SemaphoreType.DMA((3,))],
         compiler_params=params,
         cost_estimate=cost,
@@ -543,7 +550,7 @@
         match,
         keep(norm_gains),
         keep(w_head),
-        *stacks,
+        *next_weights,
     )
     return features, normals
 

time: 77.3 us -> 74.7 us (0.966)
  Pallas kernels: 76.3 us -> 73.7 us
    pallas_call x1, Pallas kernels: 67.2 us -> 65.7 us  [shards(): pl.pallas_call(first_kernel, out_shape=(jax.ShapeDtypeStruct((devices, SL...]
    pallas_call x1, Pallas kernels: 9.17 us -> 8.08 us  [shards(): pl.pallas_call(second_kernel, out_shape=(jax.ShapeDtypeStruct((rows_here,...]
where the time goes in v5:
time: 74.7 us; the launch traced here: 74.6 us
  Pallas kernels  73.7 us (99%)
  between operations  0.82 us (1%)
    pallas_call x1, Pallas kernels, shards(): pl.pallas_call(first_kernel, out_shape=(jax.ShapeDtypeStruct((devices, SL...  65.7 us
    pallas_call x1, Pallas kernels, shards(): pl.pallas_call(second_kernel, out_shape=(jax.ShapeDtypeStruct((rows_here,...  8.08 us

profile of v5, /device:TPU:1, one launch (start us, length us, event | category | flops | bytes accessed | tf_op | source)
XLA Modules:
  0.0 74.6 jit_solution(15696133426587702318)
XLA Ops:
  0.6 65.7 %first_block.1 = (bf16[128,8,512]{2,1,0:T(8,128)(2,1)S(1)}, bf16[512,1024]{1,0:T(8,128)(2,1)S(1)}, bf16[512,1536]{1,0:T(8,128)(2,1)S(1)}, bf16[512,512]{1,0:T(8,...) custom-call(s32[3,8]{1,0:T(4,128)} %bitcast.7, bf16[8,64,512]{2,1,0:T(8,128)(2,1)} %bitcast.6, ...), custom_call_target="tpu_custom_call" | custom-call | flops 6442450944 | bytes 8388608 | tf_op jit(solution)/shard_map/first_block/pallas_call | solution.py:465
  66.3 8.1 %second_block.1 = (bf16[512,512]{1,0:T(8,128)(2,1)}, f32[3,512]{1,0:T(4,128)}) custom-call(s32[3,8]{1,0:T(4,128)} %bitcast.9, bf16[1024,512]{1,0:T(8,128)(2,1)S(1)} %bitcast.5, bf16[512,1024]{1,0:T(8,128)(2,1)S(1)} %get-tuple-element.9.match, f32[4,512]{1,0:T(4,128)} %gains_hbm.3, bf16[3,512]{1,0:T(4,128)(2,1)} %head_hbm.1, ...), custom_call_target="tpu_custom_call" | custom-call | flops 6442450944 | bytes 8388608 | tf_op jit(solution)/shard_map/second_block/pallas_call | solution.py:525

commit v6 on v5

--- a/solution.py
+++ b/solution.py
@@ -327,6 +327,7 @@
     ways = range(SIDE)
     order = sorted([(dy, dx, dz, dc) for dy in ways for dx in ways for dz in ways for dc in (0, 1)], key=near)
     order.remove((0, 0, 0, 0))
+    order = [order.pop(0 if n % 4 < 3 else -1) for n in range(len(order))]
     order.append((0, 0, 0, 0))
     row = lax.broadcasted_iota(jnp.int32, (2 * SLOTS, rows_here), 0)
     for n in range(0, devices, 2):

time: 74.7 us -> 74.6 us (level)
  no operation moved by 1% of the time
where the time goes in v6:
time: 74.6 us; the launch traced here: 74.5 us
  Pallas kernels  73.7 us (99%)
  between operations  0.82 us (1%)
    pallas_call x1, Pallas kernels, shards(): pl.pallas_call(first_kernel, out_shape=(jax.ShapeDtypeStruct((devices, SL...  65.6 us
    pallas_call x1, Pallas kernels, shards(): pl.pallas_call(second_kernel, out_shape=(jax.ShapeDtypeStruct((rows_here,...  8.08 us

profile of v6, /device:TPU:1, one launch (start us, length us, event | category | flops | bytes accessed | tf_op | source)
XLA Modules:
  0.0 74.5 jit_solution(7508198024229162128)
XLA Ops:
  0.6 65.6 %first_block.1 = (bf16[128,8,512]{2,1,0:T(8,128)(2,1)S(1)}, bf16[512,1024]{1,0:T(8,128)(2,1)S(1)}, bf16[512,1536]{1,0:T(8,128)(2,1)S(1)}, bf16[512,512]{1,0:T(8,...) custom-call(s32[3,8]{1,0:T(4,128)} %bitcast.7, bf16[8,64,512]{2,1,0:T(8,128)(2,1)} %bitcast.6, ...), custom_call_target="tpu_custom_call" | custom-call | flops 6442450944 | bytes 8388608 | tf_op jit(solution)/shard_map/first_block/pallas_call | solution.py:466
  66.2 8.1 %second_block.1 = (bf16[512,512]{1,0:T(8,128)(2,1)}, f32[3,512]{1,0:T(4,128)}) custom-call(s32[3,8]{1,0:T(4,128)} %bitcast.9, bf16[1024,512]{1,0:T(8,128)(2,1)S(1)} %bitcast.5, bf16[512,1024]{1,0:T(8,128)(2,1)S(1)} %get-tuple-element.9.match, f32[4,512]{1,0:T(4,128)} %gains_hbm.3, bf16[3,512]{1,0:T(4,128)(2,1)} %head_hbm.1, ...), custom_call_target="tpu_custom_call" | custom-call | flops 6442450944 | bytes 8388608 | tf_op jit(solution)/shard_map/second_block/pallas_call | solution.py:526

commit v7 on v5

--- a/solution.py
+++ b/solution.py
@@ -140,10 +140,7 @@
         pl.semaphore_signal(barrier, inc=1, device_id=at(*peer)[0], device_id_type=MESH)
     for step in steps:
         pl.semaphore_signal(barrier, inc=1, device_id=across(step), device_id_type=MESH)
-    for load in loads:
-        load.wait()
-    rows = points[...].reshape(rows_here, channels)
-    normed[...] = norm(rows, gains[0:1]).reshape(patches, patch, channels)
+    loads[0].wait()
     lane = lax.broadcasted_iota(jnp.int32, asks.shape, 1)
     asking = jnp.full(asks.shape, -1, jnp.int32)
     named = [pattern[j, p] for p in range(patches) for j in range(pattern.shape[0])]
@@ -193,6 +190,10 @@
 
     for peer in peers:
         ask(*peer, mine[peer[0]]).start()
+    for load in loads[1:]:
+        load.wait()
+    rows = points[...].reshape(rows_here, channels)
+    normed[...] = norm(rows, gains[0:1]).reshape(patches, patch, channels)
     for early in (0, 1):
         for axis in (0, 1):
             first_step(axis, 1, early).start()

time: 74.7 us -> 75.2 us (level)
  no operation moved by 1% of the time
where the time goes in v7:
time: 75.2 us; the launch traced here: 75.1 us
  Pallas kernels  74.2 us (99%)
  between operations  0.82 us (1%)
    pallas_call x1, Pallas kernels, shards(): pl.pallas_call(first_kernel, out_shape=(jax.ShapeDtypeStruct((devices, SL...  66.1 us
    pallas_call x1, Pallas kernels, shards(): pl.pallas_call(second_kernel, out_shape=(jax.ShapeDtypeStruct((rows_here,...  8.11 us

profile of v7, /device:TPU:1, one launch (start us, length us, event | category | flops | bytes accessed | tf_op | source)
XLA Modules:
  0.0 75.1 jit_solution(11186223736685626544)
XLA Ops:
  0.6 66.1 %first_block.1 = (bf16[128,8,512]{2,1,0:T(8,128)(2,1)S(1)}, bf16[512,1024]{1,0:T(8,128)(2,1)S(1)}, bf16[512,1536]{1,0:T(8,128)(2,1)S(1)}, bf16[512,512]{1,0:T(8,...) custom-call(s32[3,8]{1,0:T(4,128)} %bitcast.7, bf16[8,64,512]{2,1,0:T(8,128)(2,1)} %bitcast.6, ...), custom_call_target="tpu_custom_call" | custom-call | flops 6442450944 | bytes 8388608 | tf_op jit(solution)/shard_map/first_block/pallas_call | solution.py:466
  66.8 8.1 %second_block.1 = (bf16[512,512]{1,0:T(8,128)(2,1)}, f32[3,512]{1,0:T(4,128)}) custom-call(s32[3,8]{1,0:T(4,128)} %bitcast.9, bf16[1024,512]{1,0:T(8,128)(2,1)S(1)} %bitcast.5, bf16[512,1024]{1,0:T(8,128)(2,1)S(1)} %get-tuple-element.9.match, f32[4,512]{1,0:T(4,128)} %gains_hbm.3, bf16[3,512]{1,0:T(4,128)(2,1)} %head_hbm.1, ...), custom_call_target="tpu_custom_call" | custom-call | flops 6442450944 | bytes 8388608 | tf_op jit(solution)/shard_map/second_block/pallas_call | solution.py:526
